TPU v7x, 256 devices: a whole 4x4x8 slice. The times are simulated.
256 devices in a mesh: box: 16 (over z, x_lo), dir: 16 (over x_hi, y, core).
Axes of the slice: x: 4 (x_hi: 2, x_lo: 2; x = x_hi * 2 + x_lo), y: 4, z: 8, core: 2. Of those that a mesh axis runs over, the one named last changes fastest.
Arguments:
- fine_out: bfloat16 [4096, 32, 512], P(('box', 'dir')), may hold values from -6 to 6
- fine_list: int32 [4096, 12], P(('box', 'dir')), may hold values from -1 to 4095, as said below
- fine_slot: int32 [4096], P('box'), may hold values from 0 to 3, as said below
- fine_translator: float32 [12, 2, 512], replicated, may hold values from -4 to 4
- theta_up_fine: bfloat16 [32, 16], replicated, may hold values from -1.5 to 1.5
- phi_up_fine: bfloat16 [64, 32], replicated, may hold values from -1 to 1
- middle_phase: float32 [4, 2048], replicated, may hold values from -3.140625 to 3.140625
- middle_list: int32 [1024, 12], P('box'), may hold values from -1 to 1023, as said below
- middle_slot: int32 [1024], P('box'), may hold values from 0 to 3, as said below
- middle_translator: float32 [12, 2, 2048], P(None, None, 'dir'), may hold values from -2 to 2
- theta_up_middle: bfloat16 [64, 32], replicated, may hold values from -1 to 1
- phi_up_middle: bfloat16 [128, 64], replicated, may hold values from -0.75 to 0.75
- coarse_phase: float32 [4, 8192], replicated, may hold values from -3.140625 to 3.140625
- coarse_list: int32 [256, 12], replicated, may hold values from -1 to 255, as said below
- coarse_translator: float32 [12, 2, 8192], P(None, None, ('box', 'dir')), may hold values from -1.25 to 1.25
Outputs:
- fine_in: bfloat16 [4096, 32, 512], P(('box', 'dir'))
- middle_in: bfloat16 [1024, 32, 2048], P('box', None, 'dir')
- coarse_in: bfloat16 [256, 32, 8192], P(None, None, ('box', 'dir'))
Inputs may be any that keep to these rules, and one draw needn't show every extreme that they name: `fine_list`: row i names distinct fine boxes j with 2 <= |j - i| <= 7 and |j // 4 - i // 4| <= 1, in any slots; -1 marks an empty slot. `middle_list`: row i names distinct middle boxes j with 2 <= |j - i| <= 7 and |j // 4 - i // 4| <= 1, in any slots; -1 marks an empty slot. `coarse_list`: row i names distinct coarse boxes j with 2 <= |j - i| <= 7 and |j // 4 - i // 4| <= 1, in any slots; -1 marks an empty slot. `fine_slot`: the parent of fine box c is middle box c // 4; each aligned group of 4 fine boxes takes each of the values 0 to 3 once. `middle_slot`: the parent of middle box m is coarse box m // 4; each aligned group of 4 middle boxes takes each of the values 0 to 3 once.
All inputs are finite; a program needn't handle non-finite values.
Results may differ from a plain program's by a relative error of at most 0.007.
Values may be sent and summed in bfloat16 or wider, within the bound.
No kernel may reach another device: no remote copies, remote signals or barrier semaphores. Data moves between devices by JAX's collectives and lax.ppermute only.
A program may use at most 64 MiB of HBM per device.

v0:
```python
import jax
import jax.numpy as jnp
from jax import lax
from jax.sharding import Mesh
from jax.sharding import PartitionSpec as P

MAX_OFFSET = 7
DIR = ("dir_0", "dir_1", "dir_2")
BOX_DIR = ("box", "dir_0", "dir_1", "dir_2")


def padded_2(shard, sides, width):
    edges = {}
    for axis, dim in sides:
        count, length = (lax.axis_size(axis), shard.shape[dim])
        up = [(i, (i + 1) % count) for i in range(count - 1)]
        last = lax.slice_in_dim(shard, length - width, length, axis=dim)
        initial = lax.slice_in_dim(shard, 0, width, axis=dim)
        edges[dim] = (
            lax.ppermute(last, axis, up),
            lax.ppermute(initial, axis, [(b, a) for a, b in up]),
        )
    done = []
    for _, dim in sides:
        low, high = edges[dim]
        around = [(width, width) if d in done else (0, 0) for d in range(shard.ndim)]
        shard = jnp.concatenate([jnp.pad(low, around), shard, jnp.pad(high, around)], axis=dim)
        done.append(dim)
    return shard


def split_up(shard, dim, count):
    before, after = (shard.shape[:dim], shard.shape[dim + 1 :])
    return jnp.moveaxis(shard.reshape(*before, count, -1, *after), dim, 0)


def joined_along(blocks, dim):
    blocks = jnp.moveaxis(blocks, 0, dim)
    dims = blocks.shape
    return blocks.reshape(*dims[:dim], dims[dim] * dims[dim + 1], *dims[dim + 2 :])


def exchange_in_order(blocks, axes, sequence):
    dims = [lax.axis_size(a) for a in axes]
    blocks = blocks.reshape(*dims, *blocks.shape[1:])
    for k in sequence:
        blocks = lax.all_to_all(blocks, axes[k], split_axis=k, concat_axis=k, tiled=True)
    return blocks.reshape(-1, *blocks.shape[len(axes) :])


def core_and_chips(shard, groups, sequence, split_dim, concat_dim):
    count = lax.axis_size(groups[0]) * lax.axis_size(groups[1])
    blocks = split_up(shard, split_dim, count)
    return joined_along(exchange_in_order(blocks, groups, sequence), concat_dim)


def padded_3(cells, sides, width):
    for axis, dim in sides:
        count = lax.axis_size(axis)
        ends = count - 1
        head = lax.slice_in_dim(cells, 0, width, axis=dim)
        tail = lax.slice_in_dim(cells, cells.shape[dim] - width, cells.shape[dim], axis=dim)
        cells = jnp.concatenate(
            [
                lax.ppermute(tail, axis, [(i, (i + 1) % count) for i in range(ends)]),
                cells,
                lax.ppermute(head, axis, [((i + 1) % count, i) for i in range(ends)]),
            ],
            axis=dim,
        )
    return cells


def joined_exchange(shard, axis, axes, splits, concats):
    sizes = [lax.axis_size(a) for a in axes]
    blocks = split_up(shard, splits[0], sizes[0])
    blocks = jnp.moveaxis(split_up(blocks, splits[1] + 1, sizes[1]), 0, 1)
    inside = blocks.shape[2:]
    blocks = blocks.reshape(-1, *inside)
    blocks = lax.all_to_all(blocks, axis, split_axis=0, concat_axis=0, tiled=True)
    blocks = joined_along(blocks.reshape(*sizes, *inside), concats[0] + 1)
    return joined_along(blocks, concats[1])


def split_times(real_part, imag_part, pattern_real, pattern_imag):
    return (
        real_part * pattern_real - imag_part * pattern_imag,
        real_part * pattern_imag + imag_part * pattern_real,
    )


def offsets_used():
    return list(range(-MAX_OFFSET, -1)) + list(range(2, MAX_OFFSET + 1))


def translate_rows(padded, entries, first_box, translator):
    row_count = entries.shape[0]
    half_size = padded.shape[1] // 2
    box_ids = first_box + jnp.arange(row_count, dtype=jnp.int32)
    real_sum = jnp.zeros((row_count, half_size, padded.shape[2]), jnp.float32)
    imag_sum = jnp.zeros((row_count, half_size, padded.shape[2]), jnp.float32)
    for slot_index, offset in enumerate(offsets_used()):
        present = jnp.any(entries == (box_ids + offset)[:, None], axis=1).astype(jnp.float32)[
            :, None, None
        ]
        source = padded[MAX_OFFSET + offset : MAX_OFFSET + offset + row_count]
        real_term, imag_term = split_times(
            translator[slot_index, 0],
            translator[slot_index, 1],
            source[:, :half_size].astype(jnp.float32),
            source[:, half_size:].astype(jnp.float32),
        )
        real_sum = real_sum + present * real_term
        imag_sum = imag_sum + present * imag_term
    return jnp.concatenate([real_sum, imag_sum], axis=1)


def interpolate(pattern, theta_matrix, phi_matrix):
    box_count, part_count = (pattern.shape[0], pattern.shape[1])
    sample_grid = pattern.reshape(
        box_count * part_count, theta_matrix.shape[1], phi_matrix.shape[1]
    )
    along_phi = jnp.einsum(
        "nap,qp->naq", sample_grid, phi_matrix, preferred_element_type=jnp.float32
    ).astype(jnp.bfloat16)
    lifted = jnp.einsum("naq,ta->ntq", along_phi, theta_matrix, preferred_element_type=jnp.float32)
    return lifted.reshape(box_count, part_count, -1)


def shift_and_sum(values, slot_ids, angles):
    choose = (slot_ids[:, None] == jnp.arange(4, dtype=jnp.int32)[None, :]).astype(jnp.float32)
    cosine = jnp.dot(choose, jnp.cos(angles), precision=lax.Precision.HIGHEST)[:, None, :]
    sine_part = jnp.dot(choose, jnp.sin(angles), precision=lax.Precision.HIGHEST)[:, None, :]
    half_size = values.shape[1] // 2
    real_term, imag_term = split_times(
        cosine, sine_part, values[:, :half_size], values[:, half_size:]
    )
    shifted = jnp.concatenate([real_term, imag_term], axis=1)
    return shifted.reshape(values.shape[0] // 4, 4, values.shape[1], values.shape[2]).sum(axis=1)


def local(
    fine_out,
    fine_list,
    fine_slot,
    fine_translator,
    theta_up_fine,
    phi_up_fine,
    middle_phase,
    middle_list,
    middle_slot,
    middle_translator,
    theta_up_middle,
    phi_up_middle,
    coarse_phase,
    coarse_list,
    coarse_translator,
):
    held_boxes = fine_out.shape[0]
    dir_rank = lax.axis_index(DIR)
    fine_pad = padded_2(fine_out, ((BOX_DIR, 0),), MAX_OFFSET)
    first_fine = lax.axis_index(BOX_DIR) * held_boxes
    fine_in = translate_rows(fine_pad, fine_list, first_fine, fine_translator).astype(jnp.bfloat16)
    parent_count = held_boxes // 4
    own_parent_slots = lax.dynamic_slice_in_dim(
        middle_slot, dir_rank * parent_count, parent_count, 0
    )
    lifted = interpolate(fine_out, theta_up_fine, phi_up_fine)
    child_slots = lax.dynamic_slice_in_dim(fine_slot, dir_rank * held_boxes, held_boxes, 0)
    parents = shift_and_sum(lifted, child_slots, middle_phase).astype(jnp.bfloat16)
    middle_out = core_and_chips(parents, (("dir_0", "dir_1"), "dir_2"), (1, 0), 2, 0)
    middle_pad = padded_3(middle_out, (("box", 0),), MAX_OFFSET)
    first_middle = lax.axis_index("box") * middle_out.shape[0]
    middle_in = translate_rows(middle_pad, middle_list, first_middle, middle_translator).astype(
        jnp.bfloat16
    )
    raised = interpolate(parents, theta_up_middle, phi_up_middle)
    coarse_own = shift_and_sum(raised, own_parent_slots, coarse_phase).astype(jnp.bfloat16)
    coarse_held = joined_exchange(coarse_own, BOX_DIR, ("box", DIR), (2, 2), (0, 0))
    box_count = lax.axis_size("box")
    dir_count_all = lax.axis_size(DIR)
    part_count = coarse_held.shape[1]
    dir_local = coarse_held.shape[2]
    ordered = coarse_held.reshape(dir_count_all, box_count, -1, part_count, dir_local)
    ordered = jnp.transpose(ordered, (1, 0, 2, 3, 4)).reshape(-1, part_count, dir_local)
    coarse_pad = jnp.pad(ordered, ((MAX_OFFSET, MAX_OFFSET), (0, 0), (0, 0)))
    coarse_in = translate_rows(coarse_pad, coarse_list, 0, coarse_translator).astype(jnp.bfloat16)
    return (fine_in, middle_in, coarse_in)


def solution(mesh):
    finer = Mesh(
        mesh.devices.reshape(mesh.shape["box"], 2, 4, 2), ("box", "dir_0", "dir_1", "dir_2")
    )
    return jax.shard_map(
        local,
        mesh=finer,
        in_specs=(
            P(BOX_DIR, None, None),
            P(BOX_DIR, None),
            P("box"),
            P(),
            P(),
            P(),
            P(),
            P("box", None),
            P("box"),
            P(None, None, DIR),
            P(),
            P(),
            P(),
            P(),
            P(None, None, BOX_DIR),
        ),
        out_specs=(P(BOX_DIR, None, None), P("box", None, DIR), P(None, None, BOX_DIR)),
        check_vma=False,
    )
```

profile of v0, /device:TPU:127, one launch (start us, length us, event | category | flops | bytes accessed | tf_op | source)
XLA Modules:
  0.0 134.0 jit_solution(15071219971808350210)
XLA Ops:
  1.4 1.2 fusion.248
  2.6 1.2 fusion.250
  3.8 2.7 %reshape.288 = bf16[512,16,32]{2,1,0:T(8,128)(2,1)S(1)} reshape(bf16[16,32,512]{2,1,0:T(8,128)(2,1)} %param.15) | data formatting | bytes 1048576 | tf_op jit(solution)/shard_map/reshape | solution.py:120
  7.5 2.9 %convolution_bitcast_fusion.1 = f32[512,32,64]{0,1,2:T(8,128)} fusion(bf16[512,16,64]{0,2,1:T(8,128)(2,1)S(1)} %fusion.2, bf16[32,16]{0,1:T(8,128)(2,1)S(1)} %copy-done.36), kind=kOutput, calls=%fused_computation.26 | convolution fusion | flops 33554432 | bytes 5243904 | tf_op jit(solution)/shard_map/naq,ta->ntq/dot_general | solution.py:126
  10.4 9.2 %copy.52 = f32[512,32,64]{2,1,0:T(8,128)} copy(f32[512,32,64]{0,1,2:T(8,128)} %convolution_bitcast_fusion.1) | data formatting | bytes 8388608 | tf_op jit(solution)/shard_map/naq,ta->ntq/transpose | solution.py:126
  19.6 7.8 %reshape.289 = f32[16,32,2048]{2,1,0:T(8,128)} reshape(f32[512,32,64]{2,1,0:T(8,128)} %copy.52) | data formatting | bytes 8388608 | tf_op jit(solution)/shard_map/reshape | solution.py:127
  27.4 2.8 %multiply_subtract_fusion.1 = (f32[16,16,2048]{2,1,0:T(8,128)S(1)}, f32[16,16,2048]{2,1,0:T(8,128)S(1)}) fusion(f32[16,32,2048]{2,1,0:T(8,128)} %reshape.289, f32[16,2048]{1,0:T(8,128)S(1)} %fusion.248, f32[16,2048]{1,0:T(8,128)S(1)} %fusion.250), kind=kLoop, calls=%fused_computation.32 | loop fusion | flops 3145728 | bytes 8650752 | tf_op jit(solution)/shard_map/sub | solution.py:87
  30.8 4.6 %all_to_all.15 = bf16[8,2,4,32,128]{4,0,3,2,1:T(8,128)(2,1)S(1)} all-to-all(bf16[8,2,4,32,128]{4,0,3,2,1:T(8,128)(2,1)S(1)} %copy.53), channel_id=1, replica_groups=mesh['box'=16,'dir_0'=2,'dir_1'=4,'dir_2'=2] {'dir_2'}, dimensions={1} | all-to-all | bytes 1048576 | tf_op jit(solution)/shard_map/all_to_all | solution.py:47
  35.3 1.3 copy.54
  36.7 6.7 %all-to-all-start.1 = ((bf16[8,2,4,32,128]{4,1,3,2,0:T(2,128)(2,1)}), bf16[8,2,4,32,128]{4,1,3,2,0:T(2,128)(2,1)}, u32[]{:S(2)}, u32[]{:S(2)}) async-start(bf16[8,2,4,32,128]{4,1,3,2,0:T(2,128)(2,1)} %copy.54), calls=%async_computation.1 | async-start | bytes 1048576 | tf_op jit(solution)/shard_map/all_to_all | solution.py:47
  44.1 5.0 %collective-permute-start = (bf16[7,32,512]{2,1,0:T(8,128)(2,1)}, bf16[7,32,512]{2,1,0:T(8,128)(2,1)}, u32[]{:S(2)}, u32[]{:S(2)}) collective-permute-start(bf16[7,32,512]{2,1,0:T(8,128)(2,1)} %get-tuple-element.53), channel_id=1, source_target_pairs={{0,1},{1,2},{2,3},{3,4},{4,5},{5,6},{6,7},{7,8},{8,9},{9,10},{10,1... | collective-permute-start | bytes 688136 | tf_op jit(solution)/shard_map/ppermute | solution.py:20
  49.1 2.1 %collective-permute-start.1 = (bf16[7,32,512]{2,1,0:T(8,128)(2,1)S(1)}, bf16[7,32,512]{2,1,0:T(8,128)(2,1)}, u32[]{:S(2)}, u32[]{:S(2)}) collective-permute-start(bf16[7,32,512]{2,1,0:T(8,128)(2,1)S(1)} %get-tuple-element.54), channel_id=1, source_target_pairs={{1,0},{2,1},{3,2},{4,3},{5,4},{6,5},{7,6},{8,7},{9,8},{10,9},{11,1... | collective-permute-start | bytes 688136 | tf_op jit(solution)/shard_map/ppermute | solution.py:21
  52.4 1.1 fusion.244
  56.6 3.0 %convolution_bitcast_fusion = f32[128,64,128]{2,1,0:T(8,128)} fusion(bf16[128,32,64]{2,1,0:T(8,128)(2,1)S(1)} %convert_element_type.583, bf16[128,64]{0,1:T(8,128)(2,1)S(1)} %copy-done, bf16[64,32]{0,1:T(8,128)(2,1)S(1)} %copy-done.8), kind=kOutput, calls=%fused_computation.25 | convolution fusion | flops 134742016 | bytes 4739072 | tf_op jit(solution)/shard_map/naq,ta->ntq/dot_general | solution.py:126
  59.6 5.0 %reshape.292 = f32[4,32,8192]{2,1,0:T(8,128)} reshape(f32[128,64,128]{2,1,0:T(8,128)} %convolution_bitcast_fusion) | data formatting | bytes 8388608 | tf_op jit(solution)/shard_map/reshape | solution.py:127
  64.6 2.8 %multiply_subtract_fusion = (f32[4,16,8192]{2,1,0:T(8,128)S(1)}, f32[4,16,8192]{2,1,0:T(8,128)S(1)}) fusion(f32[4,32,8192]{2,1,0:T(8,128)} %reshape.292, f32[4,8192]{1,0:T(4,128)S(1)} %fusion.244, f32[4,8192]{1,0:T(4,128)S(1)} %fusion.246), kind=kLoop, calls=%fused_computation.30 | loop fusion | flops 3145728 | bytes 8650752 | tf_op jit(solution)/shard_map/sub | solution.py:87
  71.0 1.2 reshape.293
  72.2 1.9 %copy.57 = bf16[16,16,1,32,32]{4,3,1,0,2:T(8,128)(2,1)} copy(bf16[16,16,1,32,32]{4,1,3,0,2:T(8,128)(2,1)S(1)} %bitcast.165) | data formatting | bytes 1048576 | tf_op jit(solution)/shard_map/transpose;transpose | solution.py:77
  74.4 4.3 %reshape.299 = bf16[256,2,512]{2,1,0:T(2,128)(2,1)} reshape(bf16[256,1,32,32]{3,2,1,0:T(8,128)(2,1)} %bitcast.166) | data formatting | bytes 1048576
  81.6 1.7 %fusion.221 = bf16[16,16,512]{2,1,0:T(8,128)(2,1)S(1)} fusion(f32[512]{0:T(512)S(1)} %bitcast.182, f32[512]{0:T(512)S(1)} %bitcast.184, f32[16]{0:T(128)S(1)} %convert_element_type.540, f32[512]{0:T(512)S(1)} %bitcast.188, f32[512]{0:T(512)S(1)} %bitcast.190, f32[16]{0:T(128)S(1)} %convert_element_type.537, f32[512]{0:T(512)S(1)} %bitcast.192, ...), kind=kLoop, calls=%fused_computation.423 | loop fusion | flops 11010048 | bytes 6603520 | tf_op jit(solution)/shard_map/convert.4
  83.2 1.7 %fusion.220 = bf16[16,16,512]{2,1,0:T(8,128)(2,1)S(1)} fusion(f32[512]{0:T(512)S(1)} %bitcast.183, f32[512]{0:T(512)S(1)} %bitcast.185, f32[16]{0:T(128)S(1)} %convert_element_type.540, f32[512]{0:T(512)S(1)} %bitcast.189, f32[512]{0:T(512)S(1)} %bitcast.191, f32[16]{0:T(128)S(1)} %convert_element_type.537, f32[512]{0:T(512)S(1)} %bitcast.193, ...), kind=kLoop, calls=%fused_computation.422 | loop fusion | flops 11010048 | bytes 6603520 | tf_op jit(solution)/shard_map/convert.5
  84.9 14.4 %all-to-all-start.2 = ((bf16[256,2,512]{2,1,0:T(2,128)(2,1)}), bf16[256,2,512]{2,1,0:T(2,128)(2,1)S(1)}, u32[]{:S(2)}, u32[]{:S(2)}) async-start(bf16[256,2,512]{2,1,0:T(2,128)(2,1)} %reshape.299), calls=%async_computation.2 | async-start | bytes 1048576 | tf_op jit(solution)/shard_map/all_to_all | solution.py:80
  99.3 1.1 copy.55
  100.5 4.8 %collective-permute-start.2 = (bf16[7,32,128]{2,1,0:T(8,128)(2,1)S(1)}, bf16[7,32,128]{2,1,0:T(8,128)(2,1)S(1)}, u32[]{:S(2)}, u32[]{:S(2)}) collective-permute-start(bf16[7,32,128]{2,1,0:T(8,128)(2,1)S(1)} %get-tuple-element.50), channel_id=1, source_target_pairs={{0,16},{16,32},{32,48},{48,64},{64,80},{80,96},{96,112},{112,128},... | collective-permute-start | bytes 172040 | tf_op jit(solution)/shard_map/ppermute | solution.py:65
  105.3 1.9 %collective-permute-start.3 = (bf16[7,32,128]{2,1,0:T(8,128)(2,1)S(1)}, bf16[7,32,128]{2,1,0:T(8,128)(2,1)S(1)}, u32[]{:S(2)}, u32[]{:S(2)}) collective-permute-start(bf16[7,32,128]{2,1,0:T(8,128)(2,1)S(1)} %get-tuple-element.49), channel_id=1, source_target_pairs={{16,0},{32,16},{48,32},{64,48},{80,64},{96,80},{112,96},{128,112},... | collective-permute-start | bytes 172040 | tf_op jit(solution)/shard_map/ppermute | solution.py:67
  108.1 1.8 %collective-permute-done.2 = bf16[7,32,128]{2,1,0:T(8,128)(2,1)S(1)} collective-permute-done((bf16[7,32,128]{2,1,0:T(8,128)(2,1)S(1)}, bf16[7,32,128]{2,1,0:T(8,128)(2,1)S(1)}, u32[]{:S(2)}, u32[]{:S(2)}) %collective-permute-start.2) | collective-permute-done | bytes 57376 | tf_op jit(solution)/shard_map/ppermute | solution.py:65
  109.9 3.9 %collective-permute-done.3 = bf16[7,32,128]{2,1,0:T(8,128)(2,1)S(1)} collective-permute-done((bf16[7,32,128]{2,1,0:T(8,128)(2,1)S(1)}, bf16[7,32,128]{2,1,0:T(8,128)(2,1)S(1)}, u32[]{:S(2)}, u32[]{:S(2)}) %collective-permute-start.3) | collective-permute-done | bytes 57376 | tf_op jit(solution)/shard_map/ppermute | solution.py:67
  113.9 5.1 %fusion.219 = bf16[64,16,128]{2,1,0:T(8,128)(2,1)S(1)} fusion(f32[128]{0:T(128)S(1)} %get-tuple-element.125, f32[128]{0:T(128)S(1)} %copy-done.11, f32[64]{0:T(128)S(1)} %convert_element_type.579, f32[128]{0:T(128)S(1)} %get-tuple-element.104, f32[128]{0:T(128)S(1)} %get-tuple-element.105, f32[64]{0:T(128)S(1)} %convert_element_type.576, ...), kind=kLoop, calls=%fused_computation.421 | loop fusion | flops 20447232 | bytes 916480 | tf_op jit(solution)/shard_map/convert.2
  119.0 5.2 %fusion.218 = bf16[64,16,128]{2,1,0:T(8,128)(2,1)S(1)} fusion(f32[128]{0:T(128)S(1)} %get-tuple-element.125, f32[128]{0:T(128)S(1)} %copy-done.11, f32[64]{0:T(128)S(1)} %convert_element_type.579, f32[128]{0:T(128)S(1)} %get-tuple-element.104, f32[128]{0:T(128)S(1)} %get-tuple-element.105, f32[64]{0:T(128)S(1)} %convert_element_type.576, ...), kind=kLoop, calls=%fused_computation.420 | loop fusion | flops 20447232 | bytes 916480 | tf_op jit(solution)/shard_map/convert.3
  126.3 1.7 %copy.59 = bf16[256,1,32,32]{0,3,2,1:T(8,128)(2,1)S(1)} copy(bf16[256,1,32,32]{3,2,1,0:T(8,128)(2,1)S(1)} %reshape.300) | data formatting | bytes 1048576 | tf_op jit(solution)/shard_map/all_to_all | solution.py:80
  128.2 2.5 %fusion.217 = bf16[256,16,32]{0,2,1:T(8,128)(2,1)S(1)} fusion(f32[32]{0:T(128)S(1)} %copy-done.34, f32[32]{0:T(128)S(1)} %copy-done.35, f32[256]{0:T(256)S(1)} %convert_element_type.619, f32[32]{0:T(128)S(1)} %copy-done.13, f32[32]{0:T(128)S(1)} %copy-done.14, f32[256]{0:T(256)S(1)} %convert_element_type.616, f32[32]{0:T(128)S(1)} %copy-done.15, ...), kind=kLoop, calls=%fused_computation.419 | loop fusion | flops 11010048 | bytes 801792 | tf_op jit(solution)/shard_map/convert
  130.7 2.5 %fusion.216 = bf16[256,16,32]{0,2,1:T(8,128)(2,1)S(1)} fusion(f32[32]{0:T(128)S(1)} %copy-done.34, f32[32]{0:T(128)S(1)} %copy-done.35, f32[256]{0:T(256)S(1)} %convert_element_type.619, f32[32]{0:T(128)S(1)} %copy-done.13, f32[32]{0:T(128)S(1)} %copy-done.14, f32[256]{0:T(256)S(1)} %convert_element_type.616, f32[32]{0:T(128)S(1)} %copy-done.15, ...), kind=kLoop, calls=%fused_computation.418 | loop fusion | flops 11010048 | bytes 801792 | tf_op jit(solution)/shard_map/convert.1
  (236 shorter events, 16.8 us)
Async XLA Ops:
  0.6 56.0 %copy-start = (bf16[128,64]{0,1:T(8,128)(2,1)S(1)}, bf16[128,64]{0,1:T(8,128)(2,1)}, u32[]{:S(2)}) copy-start(bf16[128,64]{0,1:T(8,128)(2,1)} %param.26) | copy-start | bytes 49156
  0.6 5.8 %copy-start.7 = (bf16[64,32]{0,1:T(8,128)(2,1)S(1)}, bf16[64,32]{0,1:T(8,128)(2,1)}, u32[]{:S(2)}) copy-start(bf16[64,32]{0,1:T(8,128)(2,1)} %param.20) | copy-start | bytes 12292
  30.7 12.7 %copy-start.1 = (bf16[16,32,512]{2,1,0:T(8,128)(2,1)S(1)}, bf16[16,32,512]{2,1,0:T(8,128)(2,1)}, u32[]{:S(2)}) copy-start(bf16[16,32,512]{2,1,0:T(8,128)(2,1)} %param.15) | copy-start | bytes 1572868
  35.3 16.9 %copy-start.73 = (s32[64]{0:T(128)S(1)}, s32[64]{0:T(128)}, u32[]{:S(2)}) copy-start(s32[64]{0:T(128)} %param.23) | copy-start | bytes 772
  35.3 17.0 %copy-start.2 = (f32[4,8192]{1,0:T(4,128)S(1)}, f32[4,8192]{1,0:T(4,128)}, u32[]{:S(2)}) copy-start(f32[4,8192]{1,0:T(4,128)} %param.27) | copy-start | bytes 393220
  36.7 18.0 %copy-start.5 = (f32[12,2,32]{2,1,0:T(2,128)S(1)}, f32[12,2,32]{2,1,0:T(2,128)}, u32[]{:S(2)}) copy-start(f32[12,2,32]{2,1,0:T(2,128)} %param.29) | copy-start | bytes 9220
  36.7 19.3 %copy-start.6 = (f32[12,2,128]{2,1,0:T(2,128)S(1)}, f32[12,2,128]{2,1,0:T(2,128)}, u32[]{:S(2)}) copy-start(f32[12,2,128]{2,1,0:T(2,128)} %param.24) | copy-start | bytes 36868
  36.7 19.9 %copy-start.8 = (bf16[64,32]{0,1:T(8,128)(2,1)S(1)}, bf16[64,32]{0,1:T(8,128)(2,1)}, u32[]{:S(2)}) copy-start(bf16[64,32]{0,1:T(8,128)(2,1)} %param.25) | copy-start | bytes 12292
  36.7 48.2 %all-to-all-start.1 = ((bf16[8,2,4,32,128]{4,1,3,2,0:T(2,128)(2,1)}), bf16[8,2,4,32,128]{4,1,3,2,0:T(2,128)(2,1)}, u32[]{:S(2)}, u32[]{:S(2)}) async-start(bf16[8,2,4,32,128]{4,1,3,2,0:T(2,128)(2,1)} %copy.54), calls=%async_computation.1 | async-start | bytes 1048576 | tf_op jit(solution)/shard_map/all_to_all | solution.py:47
  44.1 35.4 %collective-permute-start = (bf16[7,32,512]{2,1,0:T(8,128)(2,1)}, bf16[7,32,512]{2,1,0:T(8,128)(2,1)}, u32[]{:S(2)}, u32[]{:S(2)}) collective-permute-start(bf16[7,32,512]{2,1,0:T(8,128)(2,1)} %get-tuple-element.53), channel_id=1, source_target_pairs={{0,1},{1,2},{2,3},{3,4},{4,5},{5,6},{6,7},{7,8},{8,9},{9,10},{10,1... | collective-permute-start | bytes 688136 | tf_op jit(solution)/shard_map/ppermute | solution.py:20
  49.1 31.5 %collective-permute-start.1 = (bf16[7,32,512]{2,1,0:T(8,128)(2,1)S(1)}, bf16[7,32,512]{2,1,0:T(8,128)(2,1)}, u32[]{:S(2)}, u32[]{:S(2)}) collective-permute-start(bf16[7,32,512]{2,1,0:T(8,128)(2,1)S(1)} %get-tuple-element.54), channel_id=1, source_target_pairs={{1,0},{2,1},{3,2},{4,3},{5,4},{6,5},{7,6},{8,7},{9,8},{10,9},{11,1... | collective-permute-start | bytes 688136 | tf_op jit(solution)/shard_map/ppermute | solution.py:21
  74.2 4.9 %copy-start.65 = (pred[64]{0:T(512)(128)(4,1)S(1)}, pred[64]{0:T(512)(128)(4,1)}, u32[]{:S(2)}) copy-start(pred[64]{0:T(512)(128)(4,1)} %get-tuple-element.24) | copy-start | bytes 196
  74.3 4.9 %copy-start.64 = (pred[64]{0:T(512)(128)(4,1)S(1)}, pred[64]{0:T(512)(128)(4,1)}, u32[]{:S(2)}) copy-start(pred[64]{0:T(512)(128)(4,1)} %get-tuple-element.23) | copy-start | bytes 196
  74.3 4.9 %copy-start.63 = (pred[64]{0:T(512)(128)(4,1)S(1)}, pred[64]{0:T(512)(128)(4,1)}, u32[]{:S(2)}) copy-start(pred[64]{0:T(512)(128)(4,1)} %get-tuple-element.22) | copy-start | bytes 196
  74.3 4.9 %copy-start.62 = (pred[64]{0:T(512)(128)(4,1)S(1)}, pred[64]{0:T(512)(128)(4,1)}, u32[]{:S(2)}) copy-start(pred[64]{0:T(512)(128)(4,1)} %get-tuple-element.32) | copy-start | bytes 196
  74.3 4.9 %copy-start.61 = (pred[64]{0:T(512)(128)(4,1)S(1)}, pred[64]{0:T(512)(128)(4,1)}, u32[]{:S(2)}) copy-start(pred[64]{0:T(512)(128)(4,1)} %get-tuple-element.31) | copy-start | bytes 196
  74.3 4.9 %copy-start.60 = (pred[16]{0:T(512)(128)(4,1)S(1)}, pred[16]{0:T(512)(128)(4,1)}, u32[]{:S(2)}) copy-start(pred[16]{0:T(512)(128)(4,1)} %get-tuple-element.33) | copy-start | bytes 52
  74.3 4.9 %copy-start.59 = (pred[16]{0:T(512)(128)(4,1)S(1)}, pred[16]{0:T(512)(128)(4,1)}, u32[]{:S(2)}) copy-start(pred[16]{0:T(512)(128)(4,1)} %get-tuple-element.42) | copy-start | bytes 52
  74.3 4.9 %copy-start.58 = (pred[16]{0:T(512)(128)(4,1)S(1)}, pred[16]{0:T(512)(128)(4,1)}, u32[]{:S(2)}) copy-start(pred[16]{0:T(512)(128)(4,1)} %get-tuple-element.41) | copy-start | bytes 52
  74.3 4.9 %copy-start.57 = (pred[16]{0:T(512)(128)(4,1)S(1)}, pred[16]{0:T(512)(128)(4,1)}, u32[]{:S(2)}) copy-start(pred[16]{0:T(512)(128)(4,1)} %get-tuple-element.40) | copy-start | bytes 52
  74.3 5.0 %copy-start.56 = (pred[16]{0:T(512)(128)(4,1)S(1)}, pred[16]{0:T(512)(128)(4,1)}, u32[]{:S(2)}) copy-start(pred[16]{0:T(512)(128)(4,1)} %get-tuple-element.39) | copy-start | bytes 52
  74.3 5.0 %copy-start.55 = (pred[16]{0:T(512)(128)(4,1)S(1)}, pred[16]{0:T(512)(128)(4,1)}, u32[]{:S(2)}) copy-start(pred[16]{0:T(512)(128)(4,1)} %get-tuple-element.38) | copy-start | bytes 52
  74.4 5.0 %copy-start.54 = (pred[16]{0:T(512)(128)(4,1)S(1)}, pred[16]{0:T(512)(128)(4,1)}, u32[]{:S(2)}) copy-start(pred[16]{0:T(512)(128)(4,1)} %get-tuple-element.37) | copy-start | bytes 52
  74.4 5.0 %copy-start.53 = (pred[16]{0:T(512)(128)(4,1)S(1)}, pred[16]{0:T(512)(128)(4,1)}, u32[]{:S(2)}) copy-start(pred[16]{0:T(512)(128)(4,1)} %get-tuple-element.36) | copy-start | bytes 52
  74.4 5.0 %copy-start.52 = (pred[16]{0:T(512)(128)(4,1)S(1)}, pred[16]{0:T(512)(128)(4,1)}, u32[]{:S(2)}) copy-start(pred[16]{0:T(512)(128)(4,1)} %get-tuple-element.35) | copy-start | bytes 52
  74.4 5.0 %copy-start.51 = (pred[16]{0:T(512)(128)(4,1)S(1)}, pred[16]{0:T(512)(128)(4,1)}, u32[]{:S(2)}) copy-start(pred[16]{0:T(512)(128)(4,1)} %get-tuple-element.34) | copy-start | bytes 52
  74.4 5.0 %copy-start.50 = (pred[16]{0:T(512)(128)(4,1)S(1)}, pred[16]{0:T(512)(128)(4,1)}, u32[]{:S(2)}) copy-start(pred[16]{0:T(512)(128)(4,1)} %get-tuple-element.44) | copy-start | bytes 52
  74.4 5.0 %copy-start.49 = (pred[16]{0:T(512)(128)(4,1)S(1)}, pred[16]{0:T(512)(128)(4,1)}, u32[]{:S(2)}) copy-start(pred[16]{0:T(512)(128)(4,1)} %get-tuple-element.43) | copy-start | bytes 52
  84.9 29.0 %copy-start.11 = (f32[128]{0:T(128)S(1)}, f32[128]{0:T(128)}, u32[]{:S(2)}) copy-start(f32[128]{0:T(128)} %get-tuple-element.126) | copy-start | bytes 1540
  84.9 40.3 %all-to-all-start.2 = ((bf16[256,2,512]{2,1,0:T(2,128)(2,1)}), bf16[256,2,512]{2,1,0:T(2,128)(2,1)S(1)}, u32[]{:S(2)}, u32[]{:S(2)}) async-start(bf16[256,2,512]{2,1,0:T(2,128)(2,1)} %reshape.299), calls=%async_computation.2 | async-start | bytes 1048576 | tf_op jit(solution)/shard_map/all_to_all | solution.py:80
  100.5 9.5 %collective-permute-start.2 = (bf16[7,32,128]{2,1,0:T(8,128)(2,1)S(1)}, bf16[7,32,128]{2,1,0:T(8,128)(2,1)S(1)}, u32[]{:S(2)}, u32[]{:S(2)}) collective-permute-start(bf16[7,32,128]{2,1,0:T(8,128)(2,1)S(1)} %get-tuple-element.50), channel_id=1, source_target_pairs={{0,16},{16,32},{32,48},{48,64},{64,80},{80,96},{96,112},{112,128},... | collective-permute-start | bytes 172040 | tf_op jit(solution)/shard_map/ppermute | solution.py:65
  105.3 8.5 %collective-permute-start.3 = (bf16[7,32,128]{2,1,0:T(8,128)(2,1)S(1)}, bf16[7,32,128]{2,1,0:T(8,128)(2,1)S(1)}, u32[]{:S(2)}, u32[]{:S(2)}) collective-permute-start(bf16[7,32,128]{2,1,0:T(8,128)(2,1)S(1)} %get-tuple-element.49), channel_id=1, source_target_pairs={{16,0},{32,16},{48,32},{64,48},{80,64},{96,80},{112,96},{128,112},... | collective-permute-start | bytes 172040 | tf_op jit(solution)/shard_map/ppermute | solution.py:67
  (48 other events, 168.8 us)
where the time goes:
time: 135 us; the launch traced here: 134 us
  local copies, waits for them, and re-layouts  45.3 us (34%)
  starting transfers between devices  34.9 us (26%)
  other arithmetic  29.7 us (22%)
  matrix products  11.5 us (9%)
  waiting for transfers between devices  5.78 us (4%)
  blocking collectives  4.59 us (3%)
  between operations  2.29 us (2%)
    another operation x6, other arithmetic  18.5 us
    all_to_all x1, starting transfers between devices, joined_exchange(): lax.all_to_all(blocks, axis, split_axis=0, concat_axis=0, tiled=True)  14.4 us
    reshape x2, local copies, waits for them, and re-layouts, interpolate(): return lifted.reshape(box_count, part_count, -1)  12.8 us
    transpose x1, local copies, waits for them, and re-layouts, interpolate(): jnp.einsum('naq,ta->ntq', along_phi, theta_matrix, preferred_element_type...  9.16 us
    unnamed x153, local copies, waits for them, and re-layouts  7.44 us
    all_to_all x1, starting transfers between devices, exchange_in_order(): lax.all_to_all(blocks, axes[k], split_axis=k, concat_axis=k, tiled=True)  6.67 us
    dot_general x2, matrix products, interpolate(): jnp.einsum('naq,ta->ntq', along_phi, theta_matrix, preferred_element_type...  5.92 us
    sub x2, other arithmetic, split_times(): real_part * pattern_real - imag_part * pattern_imag  5.57 us
  transfers between devices with their start and end apart: 6, of which 2 were waited for; matrix products, arithmetic and copies ran while one was open for 34% of the time, Pallas kernels for 0%

commit v1 on v0

v1 whole, which is shorter than its diff:
```python
import functools

import jax
import jax.numpy as jnp
from jax import lax
from jax.experimental import pallas as pl
from jax.experimental.pallas import tpu as pltpu
from jax.sharding import PartitionSpec as P

REACH = 7
HALO = 4
ALL = ("box", "dir")
F32 = jnp.float32
BF16 = jnp.bfloat16
OFFSETS = list(range(-REACH, -1)) + list(range(2, REACH + 1))
VMEM = pl.BlockSpec(memory_space=pltpu.VMEM)
SMEM = pl.BlockSpec(memory_space=pltpu.SMEM)


def cos_sin(x):
    y = 0.5 * x
    z = y * y
    s = y * (
        1.0
        + z * (-1 / 6 + z * (1 / 120 + z * (-1 / 5040 + z * (1 / 362880 + z * (-1 / 39916800)))))
    )
    c = 1.0 + z * (
        -0.5
        + z * (1 / 24 + z * (-1 / 720 + z * (1 / 40320 + z * (-1 / 3628800 + z * (1 / 479001600)))))
    )
    return 1.0 - 2.0 * s * s, 2.0 * s * c


def iota(shape, dim):
    return lax.broadcasted_iota(jnp.int32, shape, dim)


def dot(a, b):
    return jnp.dot(a, b, preferred_element_type=F32)


def dot_nt(a, b):
    return lax.dot_general(a, b, (((1,), (1,)), ((), ())), preferred_element_type=F32)


def one_hot(cond):
    return cond.astype(F32).astype(BF16)


def phase_rows(phase_ref, slot_ref, first, count):
    row = iota((count, 128), 0)
    slot = jnp.zeros((count, 128), jnp.int32)
    for b in range(count):
        slot = jnp.where(row == b, slot_ref[first + b], slot)
    blocks = []
    for k in range(phase_ref.shape[1] // 128):
        part = phase_ref[:, k * 128 : (k + 1) * 128]
        rows = jnp.broadcast_to(part[3:4, :], (count, 128))
        for j in range(3):
            rows = jnp.where(slot == j, part[j : j + 1, :], rows)
        blocks.append(rows)
    return blocks


def fill_cos_sin(cs_ref, phase_ref, slot_ref, first):
    blocks = phase_rows(phase_ref, slot_ref, first, cs_ref.shape[1])
    for k, rows in enumerate(blocks):
        cos, sin = cos_sin(rows)
        cs_ref[0, :, k * 128 : (k + 1) * 128] = cos
        cs_ref[1, :, k * 128 : (k + 1) * 128] = sin


def middle_kernel(x_ref, theta_ref, phi_ref, phase_ref, slot_ref, out_ref, m_ref, cs_ref, l_ref):
    boxes, parts, dirs = x_ref.shape
    t_n, t2_n = theta_ref.shape
    p_n, q_n = phi_ref.shape
    wide = t2_n * q_n
    fill_cos_sin(cs_ref, phase_ref, slot_ref, lax.axis_index("dir") * boxes)
    spread = one_hot(iota((t2_n, wide), 1) // q_n == iota((t2_n, wide), 0))
    theta_row = dot(theta_ref[...], spread)
    repeat = one_hot(iota((q_n, wide), 1) % q_n == iota((q_n, wide), 0))
    phi_row = dot(phi_ref[...], repeat)
    for t in range(t_n):
        m_ref[t * p_n : (t + 1) * p_n, :] = (theta_row[t : t + 1, :] * phi_row).astype(BF16)
    x = x_ref[...].reshape(boxes * parts, dirs)
    half = parts // 2
    step = 256
    for n in range(wide // step):
        cols = slice(n * step, (n + 1) * step)
        l_ref[n % 2] = dot(x, m_ref[:, cols])
        for p in range(boxes // 4):
            re = jnp.zeros((half, step), F32)
            im = jnp.zeros((half, step), F32)
            for b in range(4 * p, 4 * p + 4):
                c = cs_ref[0, b : b + 1, cols]
                s = cs_ref[1, b : b + 1, cols]
                lr = l_ref[n % 2, b * parts : b * parts + half, :]
                li = l_ref[n % 2, b * parts + half : (b + 1) * parts, :]
                re = re + (c * lr - s * li)
                im = im + (c * li + s * lr)
            both = jnp.concatenate([re, im], axis=0).astype(BF16)
            for h in range(step // 128):
                out_ref[n * (step // 128) + h, p] = both[:, h * 128 : (h + 1) * 128]


def coarse_kernel(par_ref, theta_ref, phi_ref, phase_ref, slot_ref, out_ref, a_ref, cs_ref, l_ref):
    blocks, kids, parts, lanes = par_ref.shape
    t_n, t2_n = theta_ref.shape
    p_n, q_n = phi_ref.shape
    fill_cos_sin(cs_ref, phase_ref, slot_ref, lax.axis_index("dir") * kids)
    pair = lanes // p_n
    tall = one_hot(iota((lanes, p_n), 0) % p_n == iota((lanes, p_n), 1))
    phi_tall = dot(tall, phi_ref[...])
    w = jnp.concatenate(
        [jnp.where(iota((lanes, q_n), 0) // p_n == h, phi_tall, 0.0) for h in range(pair)], axis=1
    ).astype(BF16)
    e1 = one_hot(iota((t2_n * 8, t2_n), 0) // 8 == iota((t2_n * 8, t2_n), 1))
    e2 = one_hot(iota((t_n, t_n * 8), 1) // 8 == iota((t_n, t_n * 8), 0))
    stretched = dot(dot_nt(e1, theta_ref[...]).astype(BF16), e2)
    same = iota(stretched.shape, 0) % 8 == iota(stretched.shape, 1) % 8
    k8 = jnp.where(same, stretched, 0.0).astype(BF16)
    rows = kids * parts
    a_ref[...] = dot(par_ref[...].reshape(blocks * rows, lanes), w).reshape(blocks, rows, pair * q_n)
    for m in range(kids):
        for a in range(2):
            cols = []
            for r in (m * parts + 8 * a, m * parts + 16 + 8 * a):
                pieces = [
                    a_ref[t // pair, r : r + 8, (t % pair) * q_n : (t % pair + 1) * q_n]
                    for t in range(t_n)
                ]
                cols.append(jnp.concatenate(pieces, axis=0).astype(BF16))
            l_ref[m, a] = dot(k8, jnp.concatenate(cols, axis=1))
    lane = iota((8, q_n), 1)
    low = lane < 64
    even = lane % 64 < 32
    for t2 in range(t2_n):
        lanes_of = slice(t2 * q_n, (t2 + 1) * q_n)
        v = {}
        c = [cs_ref[0, m : m + 1, lanes_of] for m in range(kids)]
        s = [cs_ref[1, m : m + 1, lanes_of] for m in range(kids)]
        for a in range(2):
            re = jnp.zeros((8, q_n), F32)
            im = jnp.zeros((8, q_n), F32)
            for m in range(kids):
                lr = l_ref[m, a, t2 * 8 : t2 * 8 + 8, :q_n]
                li = l_ref[m, a, t2 * 8 : t2 * 8 + 8, q_n:]
                re = re + (c[m] * lr - s[m] * li)
                im = im + (c[m] * li + s[m] * lr)
            v[0, a] = re
            v[1, a] = im
        u = {}
        for a in range(2):
            u[0, a] = jnp.where(low, v[0, a], pltpu.roll(v[1, a], 64, 1))
            u[1, a] = jnp.where(low, pltpu.roll(v[0, a], 64, 1), v[1, a])
        for h in range(2):
            out_ref[t2 * 4 + 2 * h] = jnp.where(even, u[h, 0], pltpu.roll(u[h, 1], 32, 1)).astype(BF16)
            out_ref[t2 * 4 + 2 * h + 1] = jnp.where(
                even, pltpu.roll(u[h, 0], 96, 1), u[h, 1]
            ).astype(BF16)


def codes_by_lane(list_ref, first):
    entry = list_ref[...]
    place = entry - (first + iota(entry.shape, 1)) + REACH
    bits = jnp.where(entry >= 0, lax.shift_left(jnp.ones_like(entry), jnp.maximum(place, 0)), 0)
    row = jnp.sum(bits.astype(F32), axis=0, keepdims=True)
    return jnp.transpose(jnp.broadcast_to(row, (8, row.shape[1])))[:, :1].astype(jnp.int32)


def codes_by_row(list_ref, first):
    entry = list_ref[...]
    place = entry - (first + iota(entry.shape, 0)) + REACH
    bits = jnp.where(entry >= 0, lax.shift_left(jnp.ones_like(entry), jnp.maximum(place, 0)), 0)
    return jnp.sum(bits.astype(F32), axis=1, keepdims=True).astype(jnp.int32)


def masked(code, offset):
    return lax.bitwise_and(code, 1 << (offset + REACH)) != 0


def group_offsets(r):
    return [o for o in OFFSETS if -HALO <= r + o < 2 * HALO]


def translate_kernel(axes, by_row, x_ref, lo_ref, hi_ref, list_ref, tr_ref, out_ref, f_ref, mt_ref):
    boxes, parts, dirs = x_ref.shape
    half = parts // 2
    first = lax.axis_index(axes[0])
    for name in axes[1:]:
        first = first * lax.axis_size(name) + lax.axis_index(name)
    first = first * boxes
    code = (codes_by_row if by_row else codes_by_lane)(list_ref, first)
    code = jnp.broadcast_to(code, (boxes, 128))
    for k in range(dirs // 128):
        cols = slice(k * 128, (k + 1) * 128)
        for slot, o in enumerate(OFFSETS):
            here = masked(code, o)
            mt_ref[slot, 0, :, cols] = jnp.where(here, tr_ref[slot, 0:1, cols], 0.0)
            mt_ref[slot, 1, :, cols] = jnp.where(here, tr_ref[slot, 1:2, cols], 0.0)
    f_ref[:HALO] = lo_ref[...].astype(F32)
    f_ref[HALO : HALO + boxes] = x_ref[...].astype(F32)
    f_ref[HALO + boxes :] = hi_ref[...].astype(F32)

    def group(g, cols):
        for r in range(4):
            i = 4 * g + r
            re = jnp.zeros((half, 128), F32)
            im = jnp.zeros((half, 128), F32)
            for o in group_offsets(r):
                slot = OFFSETS.index(o)
                a = mt_ref[slot, 0, i : i + 1, cols]
                b = mt_ref[slot, 1, i : i + 1, cols]
                xr = f_ref[i + HALO + o, :half, cols]
                xi = f_ref[i + HALO + o, half:, cols]
                re = re + (a * xr - b * xi)
                im = im + (a * xi + b * xr)
            out_ref[i, :, cols] = jnp.concatenate([re, im], axis=0).astype(BF16)

    for k in range(dirs // 128):
        cols = slice(k * 128, (k + 1) * 128)

        for g in range(boxes // 4):
            group(g, cols)


def coarse_masks_kernel(list_ref, tr_ref, out_ref):
    boxes = out_ref.shape[2]
    code = jnp.broadcast_to(codes_by_lane(list_ref, 0), (boxes, 128))
    low = iota((1, 128), 1) < 64
    for slot, o in enumerate(OFFSETS):
        here = masked(code, o)
        a = jnp.concatenate([tr_ref[slot, 0:1, :]] * 4, axis=1)
        b = jnp.concatenate([tr_ref[slot, 1:2, :]] * 4, axis=1)
        b = jnp.where(low, -b, b)
        out_ref[slot, 0] = jnp.where(here, a, 0.0)
        out_ref[slot, 1] = jnp.where(here, b, 0.0)


def coarse_translate_kernel(x_ref, mt_ref, out_ref, f_ref, r_ref, y_ref):
    boxes, sub, lanes = x_ref.shape
    zero = jnp.zeros((HALO, sub, lanes), F32)
    for ref in (f_ref, r_ref):
        ref[:HALO] = zero
        ref[HALO + boxes :] = zero
    x = x_ref[...].astype(F32)
    f_ref[HALO : HALO + boxes] = x
    r_ref[HALO : HALO + boxes] = pltpu.roll(x.reshape(boxes * sub, lanes), 64, 1).reshape(x.shape)

    for g in range(boxes // 4):
        for r in range(4):
            i = 4 * g + r
            acc = jnp.zeros((sub, lanes), F32)
            for o in group_offsets(r):
                slot = OFFSETS.index(o)
                a = mt_ref[slot, 0, i : i + 1, :]
                b = mt_ref[slot, 1, i : i + 1, :]
                acc = acc + (a * f_ref[i + HALO + o] + b * r_ref[i + HALO + o])
            y_ref[i * sub : (i + 1) * sub, :] = acc
    for s in range(sub):
        turned = jnp.transpose(y_ref[pl.ds(s, boxes, stride=sub), :])
        for cb in range(4):
            out_ref[8 * cb + s] = turned[32 * cb : 32 * cb + 32, :].astype(BF16)


def call(body, out, specs, scratch, *args):
    return pl.pallas_call(
        body,
        out_shape=out,
        in_specs=specs,
        out_specs=VMEM,
        scratch_shapes=scratch,
    )(*args)


def halo(x, axes):
    count = lax.axis_size(axes)
    up = [(i, i + 1) for i in range(count - 1)]
    down = [(i + 1, i) for i in range(count - 1)]
    return lax.ppermute(x[-HALO:], axes, up), lax.ppermute(x[:HALO], axes, down)


def local(
    fine_out,
    fine_list,
    fine_slot,
    fine_translator,
    theta_up_fine,
    phi_up_fine,
    middle_phase,
    middle_list,
    middle_slot,
    middle_translator,
    theta_up_middle,
    phi_up_middle,
    coarse_phase,
    coarse_list,
    coarse_translator,
):
    shape = jax.ShapeDtypeStruct
    boxes, parts, dirs = fine_out.shape
    dir_n = lax.axis_size("dir")
    all_n = dir_n * lax.axis_size("box")
    wide = middle_phase.shape[1]
    widest = coarse_phase.shape[1]
    kids = boxes // 4
    parents = call(
        middle_kernel,
        shape((dir_n, kids, parts, wide // dir_n), BF16),
        [VMEM] * 4 + [SMEM],
        [
            pltpu.VMEM((dirs, wide), BF16),
            pltpu.VMEM((2, boxes, wide), F32),
            pltpu.VMEM((2, boxes * parts, 256), F32),
        ],
        fine_out,
        theta_up_fine.T,
        phi_up_fine.T,
        middle_phase,
        fine_slot,
    )
    t2_n = theta_up_middle.shape[0]
    q_n = phi_up_middle.shape[0]
    chunks = call(
        coarse_kernel,
        shape((all_n, 8, 128), BF16),
        [VMEM] * 4 + [SMEM],
        [
            pltpu.VMEM((dir_n, kids * parts, 2 * q_n), F32),
            pltpu.VMEM((2, kids, widest), F32),
            pltpu.VMEM((kids, 2, t2_n * 8, 2 * q_n), F32),
        ],
        parents,
        theta_up_middle.T,
        phi_up_middle.T,
        coarse_phase,
        middle_slot,
    )
    coarse_held = lax.all_to_all(chunks, ALL, split_axis=0, concat_axis=0, tiled=True)
    parents, fine_late, chunks = lax.optimization_barrier((parents, fine_out, chunks))
    middle_out = lax.all_to_all(parents, "dir", split_axis=0, concat_axis=0, tiled=True)
    middle_out = middle_out.reshape(dir_n * kids, parts, -1)
    fine_lo, fine_hi = halo(fine_late, ALL)
    fine_in = call(
        functools.partial(translate_kernel, ALL, True),
        shape(fine_out.shape, BF16),
        [VMEM] * 5,
        [
            pltpu.VMEM((boxes + 2 * HALO, parts, dirs), F32),
            pltpu.VMEM((12, 2, boxes, dirs), F32),
        ],
        fine_out,
        fine_lo,
        fine_hi,
        fine_list,
        fine_translator,
    )
    masks = call(
        coarse_masks_kernel,
        shape((12, 2, all_n, 128), F32),
        [VMEM] * 2,
        [],
        coarse_list.T,
        coarse_translator,
    )
    middle_lo, middle_hi = halo(middle_out, "box")
    held, _, lanes = middle_out.shape
    middle_in = call(
        functools.partial(translate_kernel, ("box",), False),
        shape(middle_out.shape, BF16),
        [VMEM] * 5,
        [
            pltpu.VMEM((held + 2 * HALO, parts, lanes), F32),
            pltpu.VMEM((12, 2, held, lanes), F32),
        ],
        middle_out,
        middle_lo,
        middle_hi,
        middle_list.T,
        middle_translator,
    )
    coarse_in = call(
        coarse_translate_kernel,
        shape((parts, widest // all_n, all_n), BF16),
        [VMEM] * 2,
        [
            pltpu.VMEM((all_n + 2 * HALO, 8, 128), F32),
            pltpu.VMEM((all_n + 2 * HALO, 8, 128), F32),
            pltpu.VMEM((all_n * 8, 128), F32),
        ],
        coarse_held,
        masks,
    )
    return fine_in, middle_in, jnp.transpose(coarse_in, (2, 0, 1))


def solution(mesh):
    return jax.shard_map(
        local,
        mesh=mesh,
        in_specs=(
            P(ALL, None, None),
            P(ALL, None),
            P("box"),
            P(),
            P(),
            P(),
            P(),
            P("box", None),
            P("box"),
            P(None, None, "dir"),
            P(),
            P(),
            P(),
            P(),
            P(None, None, ALL),
        ),
        out_specs=(P(ALL, None, None), P("box", None, "dir"), P(None, None, ALL)),
        check_vma=False,
    )
```

time: 135 us -> 73.5 us (0.54)
  local copies, waits for them, and re-layouts: 45.3 us -> 2.73 us
  other arithmetic: 29.7 us -> 0 us
  Pallas kernels: 0 us -> 21.9 us
  matrix products: 11.5 us -> 0 us
  blocking collectives: 4.59 us -> 15.3 us
  waiting for transfers between devices: 5.78 us -> 0.01 us
  starting transfers between devices: 34.9 us -> 32.3 us
  between operations: 2.29 us -> 0.73 us
    pallas_call x0 -> x6, Pallas kernels: none -> 21.9 us  [call(): pl.pallas_call(body, out_shape=out, in_specs=specs, out_specs=VMEM, scrat...]
    another operation x6 -> x0, other arithmetic: 18.5 us -> none
    reshape x5 -> x0, local copies, waits for them, and re-layouts: 16.8 us -> none  [the longest x2 12.8 us: interpolate(): return lifted.reshape(box_count, part_count, -1)]
    dot_general x7 -> x0, matrix products: 11.5 us -> none  [the longest x2 5.92 us: interpolate(): jnp.einsum('naq,ta->ntq', along_phi, theta_matrix, preferred_element_type...]
    all_to_all x1, blocking collectives: 4.59 us -> 15.3 us  [local(): lax.all_to_all(parents, 'dir', split_axis=0, concat_axis=0, tiled=True)]
    transpose x3 -> x0, local copies, waits for them, and re-layouts: 9.48 us -> none  [the longest x1 9.16 us: interpolate(): jnp.einsum('naq,ta->ntq', along_phi, theta_matrix, preferred_element_type...]
    all_to_all x2 -> x1, starting transfers between devices: 21 us -> 13.9 us  [local(): lax.all_to_all(chunks, ALL, split_axis=0, concat_axis=0, tiled=True)]
    ppermute x4, waiting for transfers between devices: 5.78 us -> 0.01 us  [the longest x2 0.01 us: halo(): lax.ppermute(x[:HALO], axes, down)]
  transfers between devices with their start and end apart: 6 -> 5, of which waited for: 2 -> 0; matrix products, arithmetic and copies ran while one was open for 34% -> 0% of each run, Pallas kernels for 0% -> 13%
where the time goes in v1:
time: 73.5 us; the launch traced here: 73 us
  starting transfers between devices  32.3 us (44%)
  Pallas kernels  21.9 us (30%)
  blocking collectives  15.3 us (21%)
  local copies, waits for them, and re-layouts  2.73 us (4%)
    pallas_call x6, Pallas kernels, call(): pl.pallas_call(body, out_shape=out, in_specs=specs, out_specs=VMEM, scrat...  21.9 us
    all_to_all x1, blocking collectives, local(): lax.all_to_all(parents, 'dir', split_axis=0, concat_axis=0, tiled=True)  15.3 us
    ppermute x2, starting transfers between devices, halo(): lax.ppermute(x[-HALO:], axes, up)  14.2 us
    all_to_all x1, starting transfers between devices, local(): lax.all_to_all(chunks, ALL, split_axis=0, concat_axis=0, tiled=True)  13.9 us
    ppermute x2, starting transfers between devices, halo(): lax.ppermute(x[:HALO], axes, down)  4.22 us
    unnamed x14, local copies, waits for them, and re-layouts  2.7 us
  transfers between devices with their start and end apart: 5, of which 0 were waited for; matrix products, arithmetic and copies ran while one was open for 0% of the time, Pallas kernels for 13%

profile of v1, /device:TPU:127, one launch (start us, length us, event | category | flops | bytes accessed | tf_op | source)
XLA Modules:
  0.0 73.0 jit_solution(9913566648605134652)
XLA Ops:
  0.6 0.0 copy-start
  0.6 3.5 %shard_map.166.par_ref = bf16[16,4,32,128]{3,2,1,0:T(8,128)(2,1)} custom-call(bf16[16,32,512]{2,1,0:T(8,128)(2,1)} %x_ref.3, bf16[16,32]{1,0:T(8,128)(2,1)} %bitcast.19, bf16[32,64]{1,0:T(8,128)(2,1)} %bitcast.16, f32[4,2048]{1,0:T(4,128)} %phase_ref.2, s32[256]{0:T(256)} %slot_ref.2), custom_call_target="tpu_custom_call" | custom-call | tf_op jit(solution)/shard_map/pallas_call | solution.py:267
  4.1 4.2 %shard_map.167 = bf16[256,8,128]{2,1,0:T(8,128)(2,1)} custom-call(bf16[16,4,32,128]{3,2,1,0:T(8,128)(2,1)} %shard_map.166.par_ref, bf16[32,64]{1,0:T(8,128)(2,1)} %bitcast.17, bf16[64,128]{1,0:T(8,128)(2,1)} %bitcast.14, f32[4,8192]{1,0:T(4,128)} %phase_ref.3, s32[64]{0:T(128)} %slot_ref.3), custom_call_target="tpu_custom_call" | custom-call | tf_op jit(solution)/shard_map/pallas_call | solution.py:267
  8.3 15.3 %all_to_all.10 = bf16[16,4,32,128]{3,2,1,0:T(8,128)(2,1)S(1)} all-to-all(bf16[16,4,32,128]{3,2,1,0:T(8,128)(2,1)} %shard_map.166.par_ref), channel_id=1, replica_groups=mesh['box'=16,'dir'=16] {'dir'}, dimensions={0} | all-to-all | bytes 1048576 | tf_op jit(solution)/shard_map/all_to_all | solution.py:341
  23.7 0.0 copy-start.1
  23.7 13.9 %all-to-all-start.1 = ((bf16[256,8,128]{2,1,0:T(8,128)(2,1)}), bf16[256,8,128]{2,1,0:T(8,128)(2,1)S(1)}, u32[]{:S(2)}, u32[]{:S(2)}) async-start(bf16[256,8,128]{2,1,0:T(8,128)(2,1)} %shard_map.167), calls=%async_computation.1 | async-start | bytes 1048576 | tf_op jit(solution)/shard_map/all_to_all | solution.py:339
  37.6 0.0 copy-done
  37.6 2.3 %collective-permute-start.1 = (bf16[4,32,512]{2,1,0:T(8,128)(2,1)S(1)}, bf16[4,32,512]{2,1,0:T(8,128)(2,1)S(1)}, u32[]{:S(2)}, u32[]{:S(2)}) collective-permute-start(bf16[4,32,512]{2,1,0:T(8,128)(2,1)S(1)} %get-tuple-element.9), channel_id=1, source_target_pairs={{1,0},{2,1},{3,2},{4,3},{5,4},{6,5},{7,6},{8,7},{9,8},{10,9},{11,1... | collective-permute-start | bytes 393224 | tf_op jit(solution)/shard_map/ppermute | solution.py:280
  39.9 8.7 %collective-permute-start = (bf16[4,32,512]{2,1,0:T(8,128)(2,1)S(1)}, bf16[4,32,512]{2,1,0:T(8,128)(2,1)S(1)}, u32[]{:S(2)}, u32[]{:S(2)}) collective-permute-start(bf16[4,32,512]{2,1,0:T(8,128)(2,1)S(1)} %get-tuple-element.10), channel_id=1, source_target_pairs={{0,1},{1,2},{2,3},{3,4},{4,5},{5,6},{6,7},{7,8},{8,9},{9,10},{10,1... | collective-permute-start | bytes 393224 | tf_op jit(solution)/shard_map/ppermute | solution.py:280
  48.6 1.9 %collective-permute-start.3 = (bf16[4,32,128]{2,1,0:T(8,128)(2,1)S(1)}, bf16[4,32,128]{2,1,0:T(8,128)(2,1)S(1)}, u32[]{:S(2)}, u32[]{:S(2)}) collective-permute-start(bf16[4,32,128]{2,1,0:T(8,128)(2,1)S(1)} %get-tuple-element.7), channel_id=1, source_target_pairs={{16,0},{32,16},{48,32},{64,48},{80,64},{96,80},{112,96},{128,112},... | collective-permute-start | bytes 98312 | tf_op jit(solution)/shard_map/ppermute | solution.py:280
  50.6 5.5 %collective-permute-start.2 = (bf16[4,32,128]{2,1,0:T(8,128)(2,1)S(1)}, bf16[4,32,128]{2,1,0:T(8,128)(2,1)S(1)}, u32[]{:S(2)}, u32[]{:S(2)}) collective-permute-start(bf16[4,32,128]{2,1,0:T(8,128)(2,1)S(1)} %get-tuple-element.8), channel_id=1, source_target_pairs={{0,16},{16,32},{32,48},{48,64},{64,80},{80,96},{96,112},{112,128},... | collective-permute-start | bytes 98312 | tf_op jit(solution)/shard_map/ppermute | solution.py:280
  56.1 3.0 %shard_map.170.mt_ref = f32[12,2,256,128]{3,2,1,0:T(8,128)} custom-call(s32[12,256]{1,0:T(8,128)} %bitcast.15, f32[12,2,32]{2,1,0:T(2,128)} %tr_ref.5), custom_call_target="tpu_custom_call" | custom-call | tf_op jit(solution)/shard_map/pallas_call | solution.py:267
  59.0 0.0 collective-permute-done.1.hi_ref
  59.0 0.0 copy-start.3
  59.0 0.0 collective-permute-done.lo_ref
  59.1 0.6 copy-done.3
  59.7 0.0 copy-start.4
  59.7 0.7 copy-done.4
  60.3 3.4 %shard_map.168 = bf16[16,32,512]{2,1,0:T(8,128)(2,1)} custom-call(bf16[16,32,512]{2,1,0:T(8,128)(2,1)} %x_ref.3, bf16[4,32,512]{2,1,0:T(8,128)(2,1)} %copy-done.4, bf16[4,32,512]{2,1,0:T(8,128)(2,1)} %copy-done.3, s32[16,12]{1,0:T(8,128)} %list_ref.1, f32[12,2,512]{2,1,0:T(2,128)} %tr_ref.3), custom_call_target="tpu_custom_call" | custom-call | tf_op jit(solution)/shard_map/pallas_call | solution.py:267
  63.7 0.0 collective-permute-done.3.hi_ref
  63.7 0.0 copy-start.5
  63.7 0.0 collective-permute-done.2.lo_ref
  63.7 0.0 copy-start.6
  63.7 0.0 copy-done.1
  63.8 0.6 copy-done.5
  64.3 0.0 copy-done.6
  64.3 3.3 %shard_map.169 = bf16[64,32,128]{2,1,0:T(8,128)(2,1)} custom-call(bf16[64,32,128]{2,1,0:T(8,128)(2,1)} %bitcast.12, bf16[4,32,128]{2,1,0:T(8,128)(2,1)} %copy-done.6, bf16[4,32,128]{2,1,0:T(8,128)(2,1)} %copy-done.5, s32[12,64]{1,0:T(8,128)} %bitcast.18, f32[12,2,128]{2,1,0:T(2,128)} %tr_ref.4), custom_call_target="tpu_custom_call" | custom-call | tf_op jit(solution)/shard_map/pallas_call | solution.py:267
  67.7 0.0 all-to-all-done.1.x_ref
  67.7 0.0 copy-start.2
  67.7 0.8 %copy-done.2 = bf16[256,8,128]{2,1,0:T(8,128)(2,1)} copy-done((bf16[256,8,128]{2,1,0:T(8,128)(2,1)}, bf16[256,8,128]{2,1,0:T(8,128)(2,1)S(1)}, u32[]{:S(2)}) %copy-start.2) | copy-done | bytes 524312
  68.5 4.5 %shard_map.171 = bf16[32,32,256]{2,1,0:T(8,128)(2,1)} custom-call(bf16[256,8,128]{2,1,0:T(8,128)(2,1)} %copy-done.2, f32[12,2,256,128]{3,2,1,0:T(8,128)} %shard_map.170.mt_ref), custom_call_target="tpu_custom_call" | custom-call | tf_op jit(solution)/shard_map/pallas_call | solution.py:267
  (2 shorter events, 0.0 us)
Async XLA Ops:
  0.6 37.0 %copy-start = (bf16[16,32,512]{2,1,0:T(8,128)(2,1)S(1)}, bf16[16,32,512]{2,1,0:T(8,128)(2,1)}, u32[]{:S(2)}) copy-start(bf16[16,32,512]{2,1,0:T(8,128)(2,1)} %x_ref.3) | copy-start | bytes 1572868
  23.7 40.1 %copy-start.1 = (bf16[16,4,32,128]{3,2,1,0:T(8,128)(2,1)}, bf16[16,4,32,128]{3,2,1,0:T(8,128)(2,1)S(1)}, u32[]{:S(2)}) copy-start(bf16[16,4,32,128]{3,2,1,0:T(8,128)(2,1)S(1)} %all_to_all.10) | copy-start | bytes 1572868
  23.7 44.0 %all-to-all-start.1 = ((bf16[256,8,128]{2,1,0:T(8,128)(2,1)}), bf16[256,8,128]{2,1,0:T(8,128)(2,1)S(1)}, u32[]{:S(2)}, u32[]{:S(2)}) async-start(bf16[256,8,128]{2,1,0:T(8,128)(2,1)} %shard_map.167), calls=%async_computation.1 | async-start | bytes 1048576 | tf_op jit(solution)/shard_map/all_to_all | solution.py:339
  37.6 21.4 %collective-permute-start.1 = (bf16[4,32,512]{2,1,0:T(8,128)(2,1)S(1)}, bf16[4,32,512]{2,1,0:T(8,128)(2,1)S(1)}, u32[]{:S(2)}, u32[]{:S(2)}) collective-permute-start(bf16[4,32,512]{2,1,0:T(8,128)(2,1)S(1)} %get-tuple-element.9), channel_id=1, source_target_pairs={{1,0},{2,1},{3,2},{4,3},{5,4},{6,5},{7,6},{8,7},{9,8},{10,9},{11,1... | collective-permute-start | bytes 393224 | tf_op jit(solution)/shard_map/ppermute | solution.py:280
  39.9 19.1 %collective-permute-start = (bf16[4,32,512]{2,1,0:T(8,128)(2,1)S(1)}, bf16[4,32,512]{2,1,0:T(8,128)(2,1)S(1)}, u32[]{:S(2)}, u32[]{:S(2)}) collective-permute-start(bf16[4,32,512]{2,1,0:T(8,128)(2,1)S(1)} %get-tuple-element.10), channel_id=1, source_target_pairs={{0,1},{1,2},{2,3},{3,4},{4,5},{5,6},{6,7},{7,8},{8,9},{9,10},{10,1... | collective-permute-start | bytes 393224 | tf_op jit(solution)/shard_map/ppermute | solution.py:280
  48.6 15.1 %collective-permute-start.3 = (bf16[4,32,128]{2,1,0:T(8,128)(2,1)S(1)}, bf16[4,32,128]{2,1,0:T(8,128)(2,1)S(1)}, u32[]{:S(2)}, u32[]{:S(2)}) collective-permute-start(bf16[4,32,128]{2,1,0:T(8,128)(2,1)S(1)} %get-tuple-element.7), channel_id=1, source_target_pairs={{16,0},{32,16},{48,32},{64,48},{80,64},{96,80},{112,96},{128,112},... | collective-permute-start | bytes 98312 | tf_op jit(solution)/shard_map/ppermute | solution.py:280
  50.6 13.2 %collective-permute-start.2 = (bf16[4,32,128]{2,1,0:T(8,128)(2,1)S(1)}, bf16[4,32,128]{2,1,0:T(8,128)(2,1)S(1)}, u32[]{:S(2)}, u32[]{:S(2)}) collective-permute-start(bf16[4,32,128]{2,1,0:T(8,128)(2,1)S(1)} %get-tuple-element.8), channel_id=1, source_target_pairs={{0,16},{16,32},{32,48},{48,64},{64,80},{80,96},{96,112},{112,128},... | collective-permute-start | bytes 98312 | tf_op jit(solution)/shard_map/ppermute | solution.py:280
  59.0 0.6 copy-start.3
  59.7 0.7 copy-start.4
  63.7 0.6 copy-start.5
  63.7 0.6 copy-start.6
  67.7 0.8 %copy-start.2 = (bf16[256,8,128]{2,1,0:T(8,128)(2,1)}, bf16[256,8,128]{2,1,0:T(8,128)(2,1)S(1)}, u32[]{:S(2)}) copy-start(bf16[256,8,128]{2,1,0:T(8,128)(2,1)S(1)} %all-to-all-done.1.x_ref) | copy-start | bytes 1572868

commit v2 on v1

--- a/solution.py
+++ b/solution.py
@@ -6,6 +6,7 @@
 from jax.experimental import pallas as pl
 from jax.experimental.pallas import tpu as pltpu
 from jax.sharding import PartitionSpec as P
+
 
 REACH = 7
 HALO = 4
@@ -263,13 +264,18 @@
             out_ref[8 * cb + s] = turned[32 * cb : 32 * cb + 32, :].astype(BF16)
 
 
-def call(body, out, specs, scratch, *args):
+def near(x):
+    return pltpu.with_memory_space_constraint(x, pltpu.VMEM)
+
+
+def call(body, out, specs, scratch, *args, limit=24 << 20):
     return pl.pallas_call(
         body,
         out_shape=out,
         in_specs=specs,
         out_specs=VMEM,
         scratch_shapes=scratch,
+        compiler_params=pltpu.CompilerParams(vmem_limit_bytes=limit),
     )(*args)
 
 
@@ -306,7 +312,7 @@
     kids = boxes // 4
     parents = call(
         middle_kernel,
-        shape((dir_n, kids, parts, wide // dir_n), BF16),
+        pltpu.VMEM((dir_n, kids, parts, wide // dir_n), BF16),
         [VMEM] * 4 + [SMEM],
         [
             pltpu.VMEM((dirs, wide), BF16),
@@ -318,26 +324,27 @@
         phi_up_fine.T,
         middle_phase,
         fine_slot,
+        limit=60 * 1024 * 1024,
     )
     t2_n = theta_up_middle.shape[0]
     q_n = phi_up_middle.shape[0]
-    chunks = call(
-        coarse_kernel,
-        shape((all_n, 8, 128), BF16),
+    chunks = call(coarse_kernel,
+        pltpu.VMEM((all_n, 8, 128), BF16),
         [VMEM] * 4 + [SMEM],
         [
             pltpu.VMEM((dir_n, kids * parts, 2 * q_n), F32),
             pltpu.VMEM((2, kids, widest), F32),
             pltpu.VMEM((kids, 2, t2_n * 8, 2 * q_n), F32),
         ],
-        parents,
+        near(parents),
         theta_up_middle.T,
         phi_up_middle.T,
         coarse_phase,
         middle_slot,
+        limit=60 * 1024 * 1024,
     )
     coarse_held = lax.all_to_all(chunks, ALL, split_axis=0, concat_axis=0, tiled=True)
-    parents, fine_late, chunks = lax.optimization_barrier((parents, fine_out, chunks))
+    fine_late = fine_out
     middle_out = lax.all_to_all(parents, "dir", split_axis=0, concat_axis=0, tiled=True)
     middle_out = middle_out.reshape(dir_n * kids, parts, -1)
     fine_lo, fine_hi = halo(fine_late, ALL)
@@ -350,14 +357,14 @@
             pltpu.VMEM((12, 2, boxes, dirs), F32),
         ],
         fine_out,
-        fine_lo,
-        fine_hi,
+        near(fine_lo),
+        near(fine_hi),
         fine_list,
         fine_translator,
     )
     masks = call(
         coarse_masks_kernel,
-        shape((12, 2, all_n, 128), F32),
+        pltpu.VMEM((12, 2, all_n, 128), F32),
         [VMEM] * 2,
         [],
         coarse_list.T,
@@ -365,17 +372,16 @@
     )
     middle_lo, middle_hi = halo(middle_out, "box")
     held, _, lanes = middle_out.shape
-    middle_in = call(
-        functools.partial(translate_kernel, ("box",), False),
+    middle_in = call(functools.partial(translate_kernel, ("box",), False),
         shape(middle_out.shape, BF16),
         [VMEM] * 5,
         [
             pltpu.VMEM((held + 2 * HALO, parts, lanes), F32),
             pltpu.VMEM((12, 2, held, lanes), F32),
         ],
-        middle_out,
-        middle_lo,
-        middle_hi,
+        near(middle_out),
+        near(middle_lo),
+        near(middle_hi),
         middle_list.T,
         middle_translator,
     )
@@ -388,8 +394,8 @@
             pltpu.VMEM((all_n + 2 * HALO, 8, 128), F32),
             pltpu.VMEM((all_n * 8, 128), F32),
         ],
-        coarse_held,
-        masks,
+        near(coarse_held),
+        near(masks),
     )
     return fine_in, middle_in, jnp.transpose(coarse_in, (2, 0, 1))
 

time: 73.5 us -> 63.2 us (0.86)
  blocking collectives: 15.3 us -> 0 us
  starting transfers between devices: 32.3 us -> 40.7 us
  Pallas kernels: 21.9 us -> 16.4 us
  waiting for transfers between devices: 0.01 us -> 3.74 us
  local copies, waits for them, and re-layouts: 2.73 us -> 1.11 us
    all_to_all x1 -> x0, blocking collectives: 15.3 us -> none  [local(): lax.all_to_all(parents, 'dir', split_axis=0, concat_axis=0, tiled=True)]
    all_to_all x0 -> x1, starting transfers between devices: none -> 7.39 us  [local(): lax.all_to_all(parents, 'dir', split_axis=0, concat_axis=0, tiled=True)]
    pallas_call x6, Pallas kernels: 21.9 us -> 16.4 us  [call(): pl.pallas_call(body, out_shape=out, in_specs=specs, out_specs=VMEM, scrat...]
    all_to_all x0 -> x1, waiting for transfers between devices: none -> 3.72 us  [local(): lax.all_to_all(parents, 'dir', split_axis=0, concat_axis=0, tiled=True)]
    unnamed x14 -> x20, local copies, waits for them, and re-layouts: 2.7 us -> 1.08 us
    all_to_all x1, starting transfers between devices: 13.9 us -> 14.9 us  [local(): lax.all_to_all(chunks, ALL, split_axis=0, concat_axis=0, tiled=True)]
  transfers between devices with their start and end apart: 5 -> 6, of which waited for: 0 -> 1; matrix products, arithmetic and copies ran while one was open for 0% -> 0% of each run, Pallas kernels for 13% -> 15%
where the time goes in v2:
time: 63.2 us; the launch traced here: 62.7 us
  starting transfers between devices  40.7 us (64%)
  Pallas kernels  16.4 us (26%)
  waiting for transfers between devices  3.74 us (6%)
  local copies, waits for them, and re-layouts  1.11 us (2%)
  between operations  0.84 us (1%)
    pallas_call x6, Pallas kernels, call(): pl.pallas_call(body, out_shape=out, in_specs=specs, out_specs=VMEM, scrat...  16.4 us
    all_to_all x1, starting transfers between devices, local(): lax.all_to_all(chunks, ALL, split_axis=0, concat_axis=0, tiled=True)  14.9 us
    ppermute x2, starting transfers between devices, halo(): lax.ppermute(x[-HALO:], axes, up)  14.2 us
    all_to_all x1, starting transfers between devices, local(): lax.all_to_all(parents, 'dir', split_axis=0, concat_axis=0, tiled=True)  7.39 us
    ppermute x2, starting transfers between devices, halo(): lax.ppermute(x[:HALO], axes, down)  4.22 us
    all_to_all x1, waiting for transfers between devices, local(): lax.all_to_all(parents, 'dir', split_axis=0, concat_axis=0, tiled=True)  3.72 us
  transfers between devices with their start and end apart: 6, of which 1 were waited for; matrix products, arithmetic and copies ran while one was open for 0% of the time, Pallas kernels for 15%

profile of v2, /device:TPU:127, one launch (start us, length us, event | category | flops | bytes accessed | tf_op | source)
XLA Modules:
  0.0 62.7 jit_solution(4139738529824865999)
XLA Ops:
  0.6 0.0 copy-start
  0.6 0.0 copy-start.6
  0.7 0.0 copy-start.5
  0.7 3.5 %shard_map.167.par_ref = bf16[16,4,32,128]{3,2,1,0:T(8,128)(2,1)} custom-call(bf16[16,32,512]{2,1,0:T(8,128)(2,1)} %x_ref.3, bf16[16,32]{1,0:T(8,128)(2,1)} %bitcast.19, bf16[32,64]{1,0:T(8,128)(2,1)} %bitcast.17, f32[4,2048]{1,0:T(4,128)} %phase_ref.2, s32[256]{0:T(256)} %slot_ref.2), custom_call_target="tpu_custom_call" | custom-call | tf_op jit(solution)/shard_map/pallas_call | solution.py:272
  4.2 7.4 %all-to-all-start = ((bf16[16,4,32,128]{3,2,1,0:T(8,128)(2,1)}), bf16[16,4,32,128]{3,2,1,0:T(8,128)(2,1)S(1)}, u32[]{:S(2)}, u32[]{:S(2)}) async-start(bf16[16,4,32,128]{3,2,1,0:T(8,128)(2,1)} %shard_map.167.par_ref), calls=%async_computation | async-start | bytes 1048576 | tf_op jit(solution)/shard_map/all_to_all | solution.py:348
  11.6 0.0 copy-start.8
  11.6 4.2 %shard_map.169 = bf16[256,8,128]{2,1,0:T(8,128)(2,1)} custom-call(bf16[16,4,32,128]{3,2,1,0:T(8,128)(2,1)} %shard_map.167.par_ref, bf16[32,64]{1,0:T(8,128)(2,1)} %bitcast.18, bf16[64,128]{1,0:T(8,128)(2,1)} %bitcast.16, f32[4,8192]{1,0:T(4,128)} %phase_ref.3, s32[64]{0:T(128)} %slot_ref.3), custom_call_target="tpu_custom_call" | custom-call | tf_op jit(solution)/shard_map/pallas_call | solution.py:272
  15.8 3.7 %all-to-all-done = bf16[16,4,32,128]{3,2,1,0:T(8,128)(2,1)S(1)} async-done(((bf16[16,4,32,128]{3,2,1,0:T(8,128)(2,1)}), bf16[16,4,32,128]{3,2,1,0:T(8,128)(2,1)S(1)}, u32[]{:S(2)}, u32[]{:S(2)}) %all-to-all-start) | async-done | bytes 524320 | tf_op jit(solution)/shard_map/all_to_all | solution.py:348
  19.5 14.9 %all-to-all-start.1 = ((bf16[256,8,128]{2,1,0:T(8,128)(2,1)}), bf16[256,8,128]{2,1,0:T(8,128)(2,1)}, u32[]{:S(2)}, u32[]{:S(2)}) async-start(bf16[256,8,128]{2,1,0:T(8,128)(2,1)} %shard_map.169), calls=%async_computation.1 | async-start | bytes 1048576 | tf_op jit(solution)/shard_map/all_to_all | solution.py:346
  34.4 0.0 copy-done
  34.5 2.3 %collective-permute-start.1 = (bf16[4,32,512]{2,1,0:T(8,128)(2,1)S(1)}, bf16[4,32,512]{2,1,0:T(8,128)(2,1)S(1)}, u32[]{:S(2)}, u32[]{:S(2)}) collective-permute-start(bf16[4,32,512]{2,1,0:T(8,128)(2,1)S(1)} %get-tuple-element.5), channel_id=1, source_target_pairs={{1,0},{2,1},{3,2},{4,3},{5,4},{6,5},{7,6},{8,7},{9,8},{10,9},{11,1... | collective-permute-start | bytes 393224 | tf_op jit(solution)/shard_map/ppermute | solution.py:286
  36.8 8.7 %collective-permute-start = (bf16[4,32,512]{2,1,0:T(8,128)(2,1)S(1)}, bf16[4,32,512]{2,1,0:T(8,128)(2,1)S(1)}, u32[]{:S(2)}, u32[]{:S(2)}) collective-permute-start(bf16[4,32,512]{2,1,0:T(8,128)(2,1)S(1)} %get-tuple-element.6), channel_id=1, source_target_pairs={{0,1},{1,2},{2,3},{3,4},{4,5},{5,6},{6,7},{7,8},{8,9},{9,10},{10,1... | collective-permute-start | bytes 393224 | tf_op jit(solution)/shard_map/ppermute | solution.py:286
  45.5 1.9 %collective-permute-start.3 = (bf16[4,32,128]{2,1,0:T(8,128)(2,1)S(1)}, bf16[4,32,128]{2,1,0:T(8,128)(2,1)S(1)}, u32[]{:S(2)}, u32[]{:S(2)}) collective-permute-start(bf16[4,32,128]{2,1,0:T(8,128)(2,1)S(1)} %get-tuple-element.3), channel_id=1, source_target_pairs={{16,0},{32,16},{48,32},{64,48},{80,64},{96,80},{112,96},{128,112},... | collective-permute-start | bytes 98312 | tf_op jit(solution)/shard_map/ppermute | solution.py:286
  47.4 5.5 %collective-permute-start.2 = (bf16[4,32,128]{2,1,0:T(8,128)(2,1)S(1)}, bf16[4,32,128]{2,1,0:T(8,128)(2,1)S(1)}, u32[]{:S(2)}, u32[]{:S(2)}) collective-permute-start(bf16[4,32,128]{2,1,0:T(8,128)(2,1)S(1)} %get-tuple-element.4), channel_id=1, source_target_pairs={{0,16},{16,32},{32,48},{48,64},{64,80},{80,96},{96,112},{112,128},... | collective-permute-start | bytes 98312 | tf_op jit(solution)/shard_map/ppermute | solution.py:286
  52.9 0.0 copy-done.2
  52.9 0.0 copy-done.6
  52.9 0.0 copy-done.5
  52.9 0.0 copy-start.3
  52.9 0.6 %shard_map.170.mt_ref = f32[12,2,256,128]{3,2,1,0:T(8,128)S(1)} custom-call(s32[12,256]{1,0:T(8,128)S(1)} %bitcast.13, f32[12,2,32]{2,1,0:T(2,128)S(1)} %copy-done.6), custom_call_target="tpu_custom_call" | custom-call | tf_op jit(solution)/shard_map/pallas_call | solution.py:272
  53.6 0.0 collective-permute-done.1.hi_ref
  53.6 0.0 collective-permute-done.lo_ref
  53.6 0.0 copy-done.4
  53.6 0.0 copy-done.8
  53.6 0.0 copy-start.1
  53.6 1.0 %copy-done.1 = bf16[16,32,512]{2,1,0:T(8,128)(2,1)S(1)} copy-done((bf16[16,32,512]{2,1,0:T(8,128)(2,1)S(1)}, bf16[16,32,512]{2,1,0:T(8,128)(2,1)}, u32[]{:S(2)}) %copy-start.1) | copy-done | bytes 524312
  54.7 2.2 %shard_map.166 = bf16[16,32,512]{2,1,0:T(8,128)(2,1)} custom-call(bf16[16,32,512]{2,1,0:T(8,128)(2,1)S(1)} %copy-done.1, bf16[4,32,512]{2,1,0:T(8,128)(2,1)S(1)} %collective-permute-done.lo_ref, bf16[4,32,512]{2,1,0:T(8,128)(2,1)S(1)} %collective-permute-done.1.hi_ref, s32[16,12]{1,0:T(8,128)S(1)} %copy-done.8, f32[12,2,512]{2,1,0:T(2,128)S(1)} %copy-done.4), custom_call_target="tpu_custom_call" | custom-call | tf_op jit(solution)/shard_map/pallas_call | solution.py:272
  56.9 0.0 collective-permute-done.3.hi_ref
  56.9 0.0 collective-permute-done.2.lo_ref
  56.9 0.0 copy-done.7
  56.9 2.3 %shard_map.168 = bf16[64,32,128]{2,1,0:T(8,128)(2,1)} custom-call(bf16[64,32,128]{2,1,0:T(8,128)(2,1)S(1)} %bitcast.12, bf16[4,32,128]{2,1,0:T(8,128)(2,1)S(1)} %collective-permute-done.2.lo_ref, bf16[4,32,128]{2,1,0:T(8,128)(2,1)S(1)} %collective-permute-done.3.hi_ref, s32[12,64]{1,0:T(8,128)S(1)} %bitcast.14, f32[12,2,128]{2,1,0:T(2,128)S(1)} %copy-done.7), custom_call_target="tpu_custom_call" | custom-call | tf_op jit(solution)/shard_map/pallas_call | solution.py:272
  59.2 0.0 all-to-all-done.1.x_ref
  59.2 3.5 %shard_map.171 = bf16[32,32,256]{2,1,0:T(8,128)(2,1)} custom-call(bf16[256,8,128]{2,1,0:T(8,128)(2,1)} %all-to-all-done.1.x_ref, f32[12,2,256,128]{3,2,1,0:T(8,128)S(1)} %shard_map.170.mt_ref), custom_call_target="tpu_custom_call" | custom-call | tf_op jit(solution)/shard_map/pallas_call | solution.py:272
  (8 shorter events, 0.0 us)
Async XLA Ops:
  0.6 33.8 %copy-start = (bf16[16,32,512]{2,1,0:T(8,128)(2,1)S(1)}, bf16[16,32,512]{2,1,0:T(8,128)(2,1)}, u32[]{:S(2)}) copy-start(bf16[16,32,512]{2,1,0:T(8,128)(2,1)} %x_ref.3) | copy-start | bytes 1572868
  0.6 52.3 %copy-start.6 = (f32[12,2,32]{2,1,0:T(2,128)S(1)}, f32[12,2,32]{2,1,0:T(2,128)}, u32[]{:S(2)}) copy-start(f32[12,2,32]{2,1,0:T(2,128)} %tr_ref.5) | copy-start | bytes 9220
  0.7 52.3 %copy-start.5 = (s32[256,12]{0,1:T(8,128)S(1)}, s32[256,12]{0,1:T(8,128)}, u32[]{:S(2)}) copy-start(s32[256,12]{0,1:T(8,128)} %param.28) | copy-start | bytes 36868
  4.2 15.3 %all-to-all-start = ((bf16[16,4,32,128]{3,2,1,0:T(8,128)(2,1)}), bf16[16,4,32,128]{3,2,1,0:T(8,128)(2,1)S(1)}, u32[]{:S(2)}, u32[]{:S(2)}) async-start(bf16[16,4,32,128]{3,2,1,0:T(8,128)(2,1)} %shard_map.167.par_ref), calls=%async_computation | async-start | bytes 1048576 | tf_op jit(solution)/shard_map/all_to_all | solution.py:348
  11.6 42.0 %copy-start.4 = (f32[12,2,512]{2,1,0:T(2,128)S(1)}, f32[12,2,512]{2,1,0:T(2,128)}, u32[]{:S(2)}) copy-start(f32[12,2,512]{2,1,0:T(2,128)} %tr_ref.3) | copy-start | bytes 147460
  11.6 42.0 %copy-start.8 = (s32[16,12]{1,0:T(8,128)S(1)}, s32[16,12]{1,0:T(8,128)}, u32[]{:S(2)}) copy-start(s32[16,12]{1,0:T(8,128)} %list_ref.1) | copy-start | bytes 2308
  15.8 41.1 %copy-start.7 = (f32[12,2,128]{2,1,0:T(2,128)S(1)}, f32[12,2,128]{2,1,0:T(2,128)}, u32[]{:S(2)}) copy-start(f32[12,2,128]{2,1,0:T(2,128)} %tr_ref.4) | copy-start | bytes 36868
  15.8 41.1 %copy-start.9 = (s32[64,12]{0,1:T(8,128)S(1)}, s32[64,12]{0,1:T(8,128)}, u32[]{:S(2)}) copy-start(s32[64,12]{0,1:T(8,128)} %param.22) | copy-start | bytes 9220
  19.5 33.4 %copy-start.2 = (bf16[16,4,32,128]{3,2,1,0:T(8,128)(2,1)}, bf16[16,4,32,128]{3,2,1,0:T(8,128)(2,1)S(1)}, u32[]{:S(2)}) copy-start(bf16[16,4,32,128]{3,2,1,0:T(8,128)(2,1)S(1)} %all-to-all-done) | copy-start | bytes 1572868
  19.5 39.7 %all-to-all-start.1 = ((bf16[256,8,128]{2,1,0:T(8,128)(2,1)}), bf16[256,8,128]{2,1,0:T(8,128)(2,1)}, u32[]{:S(2)}, u32[]{:S(2)}) async-start(bf16[256,8,128]{2,1,0:T(8,128)(2,1)} %shard_map.169), calls=%async_computation.1 | async-start | bytes 1048576 | tf_op jit(solution)/shard_map/all_to_all | solution.py:346
  34.5 19.1 %collective-permute-start.1 = (bf16[4,32,512]{2,1,0:T(8,128)(2,1)S(1)}, bf16[4,32,512]{2,1,0:T(8,128)(2,1)S(1)}, u32[]{:S(2)}, u32[]{:S(2)}) collective-permute-start(bf16[4,32,512]{2,1,0:T(8,128)(2,1)S(1)} %get-tuple-element.5), channel_id=1, source_target_pairs={{1,0},{2,1},{3,2},{4,3},{5,4},{6,5},{7,6},{8,7},{9,8},{10,9},{11,1... | collective-permute-start | bytes 393224 | tf_op jit(solution)/shard_map/ppermute | solution.py:286
  36.8 16.8 %collective-permute-start = (bf16[4,32,512]{2,1,0:T(8,128)(2,1)S(1)}, bf16[4,32,512]{2,1,0:T(8,128)(2,1)S(1)}, u32[]{:S(2)}, u32[]{:S(2)}) collective-permute-start(bf16[4,32,512]{2,1,0:T(8,128)(2,1)S(1)} %get-tuple-element.6), channel_id=1, source_target_pairs={{0,1},{1,2},{2,3},{3,4},{4,5},{5,6},{6,7},{7,8},{8,9},{9,10},{10,1... | collective-permute-start | bytes 393224 | tf_op jit(solution)/shard_map/ppermute | solution.py:286
  45.5 11.4 %collective-permute-start.3 = (bf16[4,32,128]{2,1,0:T(8,128)(2,1)S(1)}, bf16[4,32,128]{2,1,0:T(8,128)(2,1)S(1)}, u32[]{:S(2)}, u32[]{:S(2)}) collective-permute-start(bf16[4,32,128]{2,1,0:T(8,128)(2,1)S(1)} %get-tuple-element.3), channel_id=1, source_target_pairs={{16,0},{32,16},{48,32},{64,48},{80,64},{96,80},{112,96},{128,112},... | collective-permute-start | bytes 98312 | tf_op jit(solution)/shard_map/ppermute | solution.py:286
  47.4 9.5 %collective-permute-start.2 = (bf16[4,32,128]{2,1,0:T(8,128)(2,1)S(1)}, bf16[4,32,128]{2,1,0:T(8,128)(2,1)S(1)}, u32[]{:S(2)}, u32[]{:S(2)}) collective-permute-start(bf16[4,32,128]{2,1,0:T(8,128)(2,1)S(1)} %get-tuple-element.4), channel_id=1, source_target_pairs={{0,16},{16,32},{32,48},{48,64},{64,80},{80,96},{96,112},{112,128},... | collective-permute-start | bytes 98312 | tf_op jit(solution)/shard_map/ppermute | solution.py:286
  52.9 4.0 %copy-start.3 = (bf16[16,4,32,128]{3,2,1,0:T(8,128)(2,1)S(1)}, bf16[16,4,32,128]{3,2,1,0:T(8,128)(2,1)}, u32[]{:S(2)}) copy-start(bf16[16,4,32,128]{3,2,1,0:T(8,128)(2,1)} %copy-done.2) | copy-start | bytes 1572868
  53.6 1.0 %copy-start.1 = (bf16[16,32,512]{2,1,0:T(8,128)(2,1)S(1)}, bf16[16,32,512]{2,1,0:T(8,128)(2,1)}, u32[]{:S(2)}) copy-start(bf16[16,32,512]{2,1,0:T(8,128)(2,1)} %x_ref.3) | copy-start | bytes 1572868

commit v3 on v2

--- a/solution.py
+++ b/solution.py
@@ -71,7 +71,23 @@
         cs_ref[1, :, k * 128 : (k + 1) * 128] = sin
 
 
-def middle_kernel(x_ref, theta_ref, phi_ref, phase_ref, slot_ref, out_ref, m_ref, cs_ref, l_ref):
+def middle_kernel(
+    x_ref,
+    theta_ref,
+    phi_ref,
+    phase_ref,
+    slot_ref,
+    out_ref,
+    y0_ref,
+    y1_ref,
+    y2_ref,
+    y3_ref,
+    ea_ref,
+    eb_ref,
+    m_ref,
+    cs_ref,
+    l_ref,
+):
     boxes, parts, dirs = x_ref.shape
     t_n, t2_n = theta_ref.shape
     p_n, q_n = phi_ref.shape
@@ -83,25 +99,36 @@
     phi_row = dot(phi_ref[...], repeat)
     for t in range(t_n):
         m_ref[t * p_n : (t + 1) * p_n, :] = (theta_row[t : t + 1, :] * phi_row).astype(BF16)
+    mine = lax.axis_index("dir")
+    core = mine % 2
+    ea_ref[...] = x_ref[pl.ds((1 - core) * (boxes - HALO), HALO)]
+    eb_ref[...] = x_ref[pl.ds(core * (boxes - HALO), HALO)]
     x = x_ref[...].reshape(boxes * parts, dirs)
     half = parts // 2
     step = 256
-    for n in range(wide // step):
-        cols = slice(n * step, (n + 1) * step)
-        l_ref[n % 2] = dot(x, m_ref[:, cols])
+    same = jnp.broadcast_to(core, (parts, 128)) == 0
+    for e in range(wide // step):
+        n = lax.bitwise_xor(mine // 2, e)
+        cols = pl.ds(pl.multiple_of(n * step, step), step)
+        l_ref[e % 2] = dot(x, m_ref[:, cols])
         for p in range(boxes // 4):
             re = jnp.zeros((half, step), F32)
             im = jnp.zeros((half, step), F32)
             for b in range(4 * p, 4 * p + 4):
                 c = cs_ref[0, b : b + 1, cols]
                 s = cs_ref[1, b : b + 1, cols]
-                lr = l_ref[n % 2, b * parts : b * parts + half, :]
-                li = l_ref[n % 2, b * parts + half : (b + 1) * parts, :]
+                lr = l_ref[e % 2, b * parts : b * parts + half, :]
+                li = l_ref[e % 2, b * parts + half : (b + 1) * parts, :]
                 re = re + (c * lr - s * li)
                 im = im + (c * li + s * lr)
-            both = jnp.concatenate([re, im], axis=0).astype(BF16)
-            for h in range(step // 128):
-                out_ref[n * (step // 128) + h, p] = both[:, h * 128 : (h + 1) * 128]
+            both = jnp.concatenate([re, im], axis=0)
+            first = both[:, :128]
+            second = both[:, 128:]
+            out_ref[2 * n, p] = first.astype(BF16)
+            out_ref[2 * n + 1, p] = second.astype(BF16)
+            to = (y0_ref, y1_ref, y2_ref, y3_ref)[e % 4]
+            to[e // 4, 0, p] = jnp.where(same, first, second).astype(BF16)
+            to[e // 4, 1, p] = jnp.where(same, second, first).astype(BF16)
 
 
 def coarse_kernel(par_ref, theta_ref, phi_ref, phase_ref, slot_ref, out_ref, a_ref, cs_ref, l_ref):
@@ -161,6 +188,30 @@
             ).astype(BF16)
 
 
+def pack_x_kernel(y0_ref, y1_ref, y2_ref, y3_ref, out_ref):
+    for y, ref in enumerate((y0_ref, y1_ref, y2_ref, y3_ref)):
+        out_ref[y] = ref[1]
+
+
+def pack_core_kernel(y0_ref, y1_ref, y2_ref, y3_ref, x_ref, out_ref):
+    for y, ref in enumerate((y0_ref, y1_ref, y2_ref, y3_ref)):
+        out_ref[0, y] = ref[0, 1]
+        out_ref[1, y] = x_ref[y, 1]
+
+
+def gather_kernel(y0_ref, y1_ref, y2_ref, y3_ref, x_ref, c_ref, out_ref, ea_ref, eb_ref):
+    mine = lax.axis_index("dir")
+    for y, ref in enumerate((y0_ref, y1_ref, y2_ref, y3_ref)):
+        out_ref[lax.bitwise_xor(mine, 2 * y)] = ref[0, 0]
+        out_ref[lax.bitwise_xor(mine, 8 + 2 * y)] = x_ref[y, 0]
+        out_ref[lax.bitwise_xor(mine, 2 * y + 1)] = c_ref[0, y]
+        out_ref[lax.bitwise_xor(mine, 8 + 2 * y + 1)] = c_ref[1, y]
+    last = out_ref.shape[0] - 1
+    odd = lax.axis_index("box") % 2
+    ea_ref[...] = out_ref[(1 - odd) * last]
+    eb_ref[...] = out_ref[odd * last]
+
+
 def codes_by_lane(list_ref, first):
     entry = list_ref[...]
     place = entry - (first + iota(entry.shape, 1)) + REACH
@@ -184,12 +235,13 @@
     return [o for o in OFFSETS if -HALO <= r + o < 2 * HALO]
 
 
-def translate_kernel(axes, by_row, x_ref, lo_ref, hi_ref, list_ref, tr_ref, out_ref, f_ref, mt_ref):
+def translate_kernel(axes, by_row, x_ref, a_ref, b_ref, list_ref, tr_ref, out_ref, f_ref, mt_ref):
     boxes, parts, dirs = x_ref.shape
     half = parts // 2
     first = lax.axis_index(axes[0])
     for name in axes[1:]:
         first = first * lax.axis_size(name) + lax.axis_index(name)
+    odd = first % 2
     first = first * boxes
     code = (codes_by_row if by_row else codes_by_lane)(list_ref, first)
     code = jnp.broadcast_to(code, (boxes, 128))
@@ -199,9 +251,9 @@
             here = masked(code, o)
             mt_ref[slot, 0, :, cols] = jnp.where(here, tr_ref[slot, 0:1, cols], 0.0)
             mt_ref[slot, 1, :, cols] = jnp.where(here, tr_ref[slot, 1:2, cols], 0.0)
-    f_ref[:HALO] = lo_ref[...].astype(F32)
+    f_ref[pl.ds((1 - odd) * (HALO + boxes), HALO)] = a_ref[...].astype(F32)
     f_ref[HALO : HALO + boxes] = x_ref[...].astype(F32)
-    f_ref[HALO + boxes :] = hi_ref[...].astype(F32)
+    f_ref[pl.ds(odd * (HALO + boxes), HALO)] = b_ref[...].astype(F32)
 
     def group(g, cols):
         for r in range(4):
@@ -273,17 +325,22 @@
         body,
         out_shape=out,
         in_specs=specs,
-        out_specs=VMEM,
+        out_specs=jax.tree.map(lambda _: VMEM, out),
         scratch_shapes=scratch,
         compiler_params=pltpu.CompilerParams(vmem_limit_bytes=limit),
     )(*args)
 
 
-def halo(x, axes):
+def swap(x, axis, bits):
+    return lax.ppermute(x, axis, [(i, i ^ bits) for i in range(lax.axis_size(axis))])
+
+
+def halo(first, second, axes):
     count = lax.axis_size(axes)
-    up = [(i, i + 1) for i in range(count - 1)]
-    down = [(i + 1, i) for i in range(count - 1)]
-    return lax.ppermute(x[-HALO:], axes, up), lax.ppermute(x[:HALO], axes, down)
+    pairs = [(i, i + 1) for i in range(1, count - 1, 2)]
+    pairs = pairs + [(b, a) for a, b in pairs]
+    a = swap(first, axes, 1)
+    return a, lax.ppermute(second, axes, pairs)
 
 
 def local(
@@ -310,9 +367,14 @@
     wide = middle_phase.shape[1]
     widest = coarse_phase.shape[1]
     kids = boxes // 4
-    parents = call(
+    width = wide // dir_n
+    piece = (kids, parts, width)
+    edge = shape((HALO, parts, dirs), BF16)
+    parents, y0, y1, y2, y3, fine_a, fine_b = call(
         middle_kernel,
-        pltpu.VMEM((dir_n, kids, parts, wide // dir_n), BF16),
+        (pltpu.VMEM((dir_n,) + piece, BF16),)
+        + (pltpu.VMEM((dir_n // 8, 2) + piece, BF16),) * 4
+        + (edge, edge),
         [VMEM] * 4 + [SMEM],
         [
             pltpu.VMEM((dirs, wide), BF16),
@@ -326,6 +388,9 @@
         fine_slot,
         limit=60 * 1024 * 1024,
     )
+    y1 = swap(y1, "dir", 2)
+    y2 = swap(y2, "dir", 4)
+    y3 = swap(y3, "dir", 6)
     t2_n = theta_up_middle.shape[0]
     q_n = phi_up_middle.shape[0]
     chunks = call(coarse_kernel,
@@ -344,10 +409,25 @@
         limit=60 * 1024 * 1024,
     )
     coarse_held = lax.all_to_all(chunks, ALL, split_axis=0, concat_axis=0, tiled=True)
-    fine_late = fine_out
-    middle_out = lax.all_to_all(parents, "dir", split_axis=0, concat_axis=0, tiled=True)
-    middle_out = middle_out.reshape(dir_n * kids, parts, -1)
-    fine_lo, fine_hi = halo(fine_late, ALL)
+    ys = (y0, y1, y2, y3)
+    ys = tuple(near(y) for y in ys)
+    xs = call(pack_x_kernel, pltpu.VMEM((4, 2) + piece, BF16), [VMEM] * 4, [], *ys)
+    xs = swap(xs, "dir", 8)
+    cs = pltpu.VMEM((2, 4) + piece, BF16)
+    cs = call(pack_core_kernel, cs, [VMEM] * 5, [], *ys, near(xs))
+    cs = swap(cs, "dir", 1)
+    edge = shape(piece, BF16)
+    middle_out, middle_a, middle_b = call(
+        gather_kernel,
+        (pltpu.VMEM((dir_n,) + piece, BF16), edge, edge),
+        [VMEM] * 6,
+        [],
+        *ys,
+        near(xs),
+        near(cs),
+    )
+    middle_out = middle_out.reshape(dir_n * kids, parts, width)
+    fine_a, fine_b = halo(fine_a, fine_b, ALL)
     fine_in = call(
         functools.partial(translate_kernel, ALL, True),
         shape(fine_out.shape, BF16),
@@ -357,8 +437,8 @@
             pltpu.VMEM((12, 2, boxes, dirs), F32),
         ],
         fine_out,
-        near(fine_lo),
-        near(fine_hi),
+        near(fine_a),
+        near(fine_b),
         fine_list,
         fine_translator,
     )
@@ -370,7 +450,7 @@
         coarse_list.T,
         coarse_translator,
     )
-    middle_lo, middle_hi = halo(middle_out, "box")
+    middle_a, middle_b = halo(middle_a, middle_b, "box")
     held, _, lanes = middle_out.shape
     middle_in = call(functools.partial(translate_kernel, ("box",), False),
         shape(middle_out.shape, BF16),
@@ -380,8 +460,8 @@
             pltpu.VMEM((12, 2, held, lanes), F32),
         ],
         near(middle_out),
-        near(middle_lo),
-        near(middle_hi),
+        near(middle_a),
+        near(middle_b),
         middle_list.T,
         middle_translator,
     )

time: 63.2 us -> 69.1 us (1.093)
  the two profiles are of different devices: /device:TPU:127 before, /device:TPU:4 now
where the time goes in v3:
time: 69.1 us; the launch traced here: 68.8 us
  starting transfers between devices  27.2 us (39%)
  waiting for transfers between devices  24.2 us (35%)
  Pallas kernels  16.6 us (24%)
  between operations  0.81 us (1%)
    ppermute x7, waiting for transfers between devices, swap(): lax.ppermute(x, axis, [(i, i ^ bits) for i in range(lax.axis_size(axis))])  20.1 us
    pallas_call x9, Pallas kernels, call(): pl.pallas_call(body, out_shape=out, in_specs=specs, out_specs=jax.tree.ma...  16.6 us
    all_to_all x1, starting transfers between devices, local(): lax.all_to_all(chunks, ALL, split_axis=0, concat_axis=0, tiled=True)  15.7 us
    ppermute x7, starting transfers between devices, swap(): lax.ppermute(x, axis, [(i, i ^ bits) for i in range(lax.axis_size(axis))])  8.37 us
    ppermute x2, waiting for transfers between devices, halo(): return (a, lax.ppermute(second, axes, pairs))  4.09 us
    ppermute x2, starting transfers between devices, halo(): return (a, lax.ppermute(second, axes, pairs))  3.13 us
  transfers between devices with their start and end apart: 10, of which 5 were waited for; matrix products, arithmetic and copies ran while one was open for 0% of the time, Pallas kernels for 8%

profile of v3, /device:TPU:4, one launch (start us, length us, event | category | flops | bytes accessed | tf_op | source)
XLA Modules:
  0.0 68.8 jit_solution(13367472366260192490)
XLA Ops:
  0.7 3.8 %shard_map.166 = (bf16[16,4,32,128]{3,2,1,0:T(8,128)(2,1)S(1)}, bf16[2,2,4,32,128]{4,3,2,1,0:T(8,128)(2,1)S(1)}, bf16[2,2,4,32,128]{4,3,2,1,0:T(8,128)(2,1)S(1)}...) custom-call(bf16[16,32,512]{2,1,0:T(8,128)(2,1)} %x_ref.3, ...), custom_call_target="tpu_custom_call" | custom-call | tf_op jit(solution)/shard_map/pallas_call | solution.py:324
  4.5 4.1 %shard_map.172 = bf16[256,8,128]{2,1,0:T(8,128)(2,1)} custom-call(bf16[16,4,32,128]{3,2,1,0:T(8,128)(2,1)S(1)} %get-tuple-element.22.par_ref, bf16[32,64]{1,0:T(8,128)(2,1)} %bitcast.14, bf16[64,128]{1,0:T(8,128)(2,1)} %bitcast.12, f32[4,8192]{1,0:T(4,128)} %phase_ref.3, s32[64]{0:T(128)} %slot_ref.3), custom_call_target="tpu_custom_call" | custom-call | tf_op jit(solution)/shard_map/pallas_call | solution.py:324
  8.5 15.7 %all-to-all-start = ((bf16[256,8,128]{2,1,0:T(8,128)(2,1)}), bf16[256,8,128]{2,1,0:T(8,128)(2,1)}, u32[]{:S(2)}, u32[]{:S(2)}) async-start(bf16[256,8,128]{2,1,0:T(8,128)(2,1)} %shard_map.172), calls=%async_computation | async-start | bytes 1048576 | tf_op jit(solution)/shard_map/all_to_all | solution.py:411
  24.2 0.0 copy-start
  24.2 0.0 copy-start.1
  24.2 0.0 copy-start.5
  24.2 1.6 %collective-permute-start.2 = (bf16[2,2,4,32,128]{4,3,2,1,0:T(8,128)(2,1)S(1)}, bf16[2,2,4,32,128]{4,3,2,1,0:T(8,128)(2,1)S(1)}, u32[]{:S(2)}, u32[]{:S(2)}) collective-permute-start(bf16[2,2,4,32,128]{4,3,2,1,0:T(8,128)(2,1)S(1)} %get-tuple-element.16), channel_id=1, source_target_pairs={{0,2},{1,3},{2,0},{3,1},{4,6},{5,7},{6,4},{7,5},{8,10},{9,11},{10,... | collective-permute-start | bytes 393224 | tf_op jit(solution)/shard_map/ppermute | solution.py:335
  25.8 2.8 %collective-permute-start.3 = (bf16[2,2,4,32,128]{4,3,2,1,0:T(8,128)(2,1)S(1)}, bf16[2,2,4,32,128]{4,3,2,1,0:T(8,128)(2,1)S(1)}, u32[]{:S(2)}, u32[]{:S(2)}) collective-permute-start(bf16[2,2,4,32,128]{4,3,2,1,0:T(8,128)(2,1)S(1)} %get-tuple-element.17), channel_id=1, source_target_pairs={{0,4},{1,5},{2,6},{3,7},{4,0},{5,1},{6,2},{7,3},{8,12},{9,13},{10,... | collective-permute-start | bytes 393224 | tf_op jit(solution)/shard_map/ppermute | solution.py:335
  28.5 0.5 collective-permute-start.4
  29.0 4.0 %collective-permute-done.2.y1_ref = bf16[2,2,4,32,128]{4,3,2,1,0:T(8,128)(2,1)S(1)} collective-permute-done((bf16[2,2,4,32,128]{4,3,2,1,0:T(8,128)(2,1)S(1)}, bf16[2,2,4,32,128]{4,3,2,1,0:T(8,128)(2,1)S(1)}, u32[]{:S(2)}, u32[]{:S(2)}) %collective-permute-start.2) | collective-permute-done | bytes 131104 | tf_op jit(solution)/shard_map/ppermute | solution.py:335
  33.0 5.9 %collective-permute-done.3.y2_ref = bf16[2,2,4,32,128]{4,3,2,1,0:T(8,128)(2,1)S(1)} collective-permute-done((bf16[2,2,4,32,128]{4,3,2,1,0:T(8,128)(2,1)S(1)}, bf16[2,2,4,32,128]{4,3,2,1,0:T(8,128)(2,1)S(1)}, u32[]{:S(2)}, u32[]{:S(2)}) %collective-permute-start.3) | collective-permute-done | bytes 131104 | tf_op jit(solution)/shard_map/ppermute | solution.py:335
  38.9 1.9 %collective-permute-done.4.y3_ref = bf16[2,2,4,32,128]{4,3,2,1,0:T(8,128)(2,1)S(1)} collective-permute-done((bf16[2,2,4,32,128]{4,3,2,1,0:T(8,128)(2,1)S(1)}, bf16[2,2,4,32,128]{4,3,2,1,0:T(8,128)(2,1)S(1)}, u32[]{:S(2)}, u32[]{:S(2)}) %collective-permute-start.4) | collective-permute-done | bytes 131104 | tf_op jit(solution)/shard_map/ppermute | solution.py:335
  40.8 0.0 copy-start.4
  40.8 0.0 copy-start.6
  40.8 0.7 %collective-permute-start.5 = (bf16[4,2,4,32,128]{4,3,2,1,0:T(8,128)(2,1)S(1)}, bf16[4,2,4,32,128]{4,3,2,1,0:T(8,128)(2,1)S(1)}, u32[]{:S(2)}, u32[]{:S(2)}) collective-permute-start(bf16[4,2,4,32,128]{4,3,2,1,0:T(8,128)(2,1)S(1)} %shard_map.168), channel_id=1, source_target_pairs={{0,8},{1,9},{2,10},{3,11},{4,12},{5,13},{6,14},{7,15},{8,0},{9,1},... | collective-permute-start | bytes 786440 | tf_op jit(solution)/shard_map/ppermute | solution.py:335
  41.6 8.3 %collective-permute-done.5.x_ref = bf16[4,2,4,32,128]{4,3,2,1,0:T(8,128)(2,1)S(1)} collective-permute-done((bf16[4,2,4,32,128]{4,3,2,1,0:T(8,128)(2,1)S(1)}, bf16[4,2,4,32,128]{4,3,2,1,0:T(8,128)(2,1)S(1)}, u32[]{:S(2)}, u32[]{:S(2)}) %collective-permute-start.5) | collective-permute-done | bytes 262176 | tf_op jit(solution)/shard_map/ppermute | solution.py:335
  49.9 0.1 collective-permute-start.6
  50.0 0.5 collective-permute-start
  50.5 2.3 %collective-permute-start.1 = (bf16[4,32,512]{2,1,0:T(8,128)(2,1)S(1)}, bf16[4,32,512]{2,1,0:T(8,128)(2,1)S(1)}, u32[]{:S(2)}, u32[]{:S(2)}) collective-permute-start(bf16[4,32,512]{2,1,0:T(8,128)(2,1)S(1)} %copy-done.7), channel_id=1, source_target_pairs={{1,2},{3,4},{5,6},{7,8},{9,10},{11,12},{13,14},{15,16},{17,18},{19... | collective-permute-start | bytes 393224 | tf_op jit(solution)/shard_map/ppermute | solution.py:343
  52.8 0.0 collective-permute-done.6.c_ref
  52.8 0.1 shard_map.170
  52.9 2.3 %collective-permute-start.7 = (bf16[4,32,128]{2,1,0:T(8,128)(2,1)S(1)}, bf16[4,32,128]{2,1,0:T(8,128)(2,1)S(1)}, u32[]{:S(2)}, u32[]{:S(2)}) collective-permute-start(bf16[4,32,128]{2,1,0:T(8,128)(2,1)S(1)} %get-tuple-element.20), channel_id=1, source_target_pairs={{0,16},{16,0},{32,48},{48,32},{64,80},{80,64},{96,112},{112,96},{1... | collective-permute-start | bytes 98312 | tf_op jit(solution)/shard_map/ppermute | solution.py:335
  55.1 0.8 %collective-permute-start.8 = (bf16[4,32,128]{2,1,0:T(8,128)(2,1)S(1)}, bf16[4,32,128]{2,1,0:T(8,128)(2,1)S(1)}, u32[]{:S(2)}, u32[]{:S(2)}) collective-permute-start(bf16[4,32,128]{2,1,0:T(8,128)(2,1)S(1)} %get-tuple-element.21), channel_id=1, source_target_pairs={{16,32},{48,64},{80,96},{112,128},{144,160},{176,192},{208,224},{3... | collective-permute-start | bytes 98312 | tf_op jit(solution)/shard_map/ppermute | solution.py:343
  56.0 0.6 shard_map.173.mt_ref
  56.6 0.0 collective-permute-done.a_ref
  56.6 4.1 %collective-permute-done.1.b_ref = bf16[4,32,512]{2,1,0:T(8,128)(2,1)S(1)} collective-permute-done((bf16[4,32,512]{2,1,0:T(8,128)(2,1)S(1)}, bf16[4,32,512]{2,1,0:T(8,128)(2,1)S(1)}, u32[]{:S(2)}, u32[]{:S(2)}) %collective-permute-start.1) | collective-permute-done | bytes 131104 | tf_op jit(solution)/shard_map/ppermute | solution.py:343
  60.7 2.3 %shard_map.167 = bf16[16,32,512]{2,1,0:T(8,128)(2,1)} custom-call(bf16[16,32,512]{2,1,0:T(8,128)(2,1)S(1)} %copy-done, bf16[4,32,512]{2,1,0:T(8,128)(2,1)S(1)} %collective-permute-done.a_ref, bf16[4,32,512]{2,1,0:T(8,128)(2,1)S(1)} %collective-permute-done.1.b_ref, s32[16,12]{1,0:T(8,128)S(1)} %copy-done.5, f32[12,2,512]{2,1,0:T(2,128)S(1)} %copy-done.1), custom_call_target="tpu_custom_call" | custom-call | tf_op jit(solution)/shard_map/pallas_call | solution.py:324
  63.0 0.0 collective-permute-done.7.a_ref
  63.0 0.0 collective-permute-done.8.b_ref
  63.0 2.3 %shard_map.171 = bf16[64,32,128]{2,1,0:T(8,128)(2,1)} custom-call(bf16[64,32,128]{2,1,0:T(8,128)(2,1)S(1)} %bitcast.8, bf16[4,32,128]{2,1,0:T(8,128)(2,1)S(1)} %collective-permute-done.7.a_ref, bf16[4,32,128]{2,1,0:T(8,128)(2,1)S(1)} %collective-permute-done.8.b_ref, s32[12,64]{1,0:T(8,128)S(1)} %bitcast.10, f32[12,2,128]{2,1,0:T(2,128)S(1)} %copy-done.4), custom_call_target="tpu_custom_call" | custom-call | tf_op jit(solution)/shard_map/pallas_call | solution.py:324
  65.3 0.0 all-to-all-done.x_ref
  65.3 3.5 %shard_map.174 = bf16[32,32,256]{2,1,0:T(8,128)(2,1)} custom-call(bf16[256,8,128]{2,1,0:T(8,128)(2,1)} %all-to-all-done.x_ref, f32[12,2,256,128]{3,2,1,0:T(8,128)S(1)} %shard_map.173.mt_ref), custom_call_target="tpu_custom_call" | custom-call | tf_op jit(solution)/shard_map/pallas_call | solution.py:324
  (15 shorter events, 0.1 us)
Async XLA Ops:
  0.6 55.3 %copy-start.3 = (f32[12,2,32]{2,1,0:T(2,128)S(1)}, f32[12,2,32]{2,1,0:T(2,128)}, u32[]{:S(2)}) copy-start(f32[12,2,32]{2,1,0:T(2,128)} %tr_ref.5) | copy-start | bytes 9220
  0.6 55.3 %copy-start.2 = (s32[256,12]{0,1:T(8,128)S(1)}, s32[256,12]{0,1:T(8,128)}, u32[]{:S(2)}) copy-start(s32[256,12]{0,1:T(8,128)} %param.28) | copy-start | bytes 36868
  4.4 45.5 %copy-start.8 = (bf16[4,32,512]{2,1,0:T(8,128)(2,1)S(1)}, bf16[4,32,512]{2,1,0:T(8,128)(2,1)}, u32[]{:S(2)}) copy-start(bf16[4,32,512]{2,1,0:T(8,128)(2,1)} %get-tuple-element.13) | copy-start | bytes 393220
  4.4 46.0 %copy-start.7 = (bf16[4,32,512]{2,1,0:T(8,128)(2,1)S(1)}, bf16[4,32,512]{2,1,0:T(8,128)(2,1)}, u32[]{:S(2)}) copy-start(bf16[4,32,512]{2,1,0:T(8,128)(2,1)} %get-tuple-element.14) | copy-start | bytes 393220
  8.5 56.7 %all-to-all-start = ((bf16[256,8,128]{2,1,0:T(8,128)(2,1)}), bf16[256,8,128]{2,1,0:T(8,128)(2,1)}, u32[]{:S(2)}, u32[]{:S(2)}) async-start(bf16[256,8,128]{2,1,0:T(8,128)(2,1)} %shard_map.172), calls=%async_computation | async-start | bytes 1048576 | tf_op jit(solution)/shard_map/all_to_all | solution.py:411
  24.2 36.5 %copy-start = (bf16[16,32,512]{2,1,0:T(8,128)(2,1)S(1)}, bf16[16,32,512]{2,1,0:T(8,128)(2,1)}, u32[]{:S(2)}) copy-start(bf16[16,32,512]{2,1,0:T(8,128)(2,1)} %x_ref.3) | copy-start | bytes 1572868
  24.2 36.5 %copy-start.1 = (f32[12,2,512]{2,1,0:T(2,128)S(1)}, f32[12,2,512]{2,1,0:T(2,128)}, u32[]{:S(2)}) copy-start(f32[12,2,512]{2,1,0:T(2,128)} %tr_ref.3) | copy-start | bytes 147460
  24.2 36.5 %copy-start.5 = (s32[16,12]{1,0:T(8,128)S(1)}, s32[16,12]{1,0:T(8,128)}, u32[]{:S(2)}) copy-start(s32[16,12]{1,0:T(8,128)} %list_ref.1) | copy-start | bytes 2308
  24.2 8.8 %collective-permute-start.2 = (bf16[2,2,4,32,128]{4,3,2,1,0:T(8,128)(2,1)S(1)}, bf16[2,2,4,32,128]{4,3,2,1,0:T(8,128)(2,1)S(1)}, u32[]{:S(2)}, u32[]{:S(2)}) collective-permute-start(bf16[2,2,4,32,128]{4,3,2,1,0:T(8,128)(2,1)S(1)} %get-tuple-element.16), channel_id=1, source_target_pairs={{0,2},{1,3},{2,0},{3,1},{4,6},{5,7},{6,4},{7,5},{8,10},{9,11},{10,... | collective-permute-start | bytes 393224 | tf_op jit(solution)/shard_map/ppermute | solution.py:335
  25.8 13.1 %collective-permute-start.3 = (bf16[2,2,4,32,128]{4,3,2,1,0:T(8,128)(2,1)S(1)}, bf16[2,2,4,32,128]{4,3,2,1,0:T(8,128)(2,1)S(1)}, u32[]{:S(2)}, u32[]{:S(2)}) collective-permute-start(bf16[2,2,4,32,128]{4,3,2,1,0:T(8,128)(2,1)S(1)} %get-tuple-element.17), channel_id=1, source_target_pairs={{0,4},{1,5},{2,6},{3,7},{4,0},{5,1},{6,2},{7,3},{8,12},{9,13},{10,... | collective-permute-start | bytes 393224 | tf_op jit(solution)/shard_map/ppermute | solution.py:335
  28.5 12.2 %collective-permute-start.4 = (bf16[2,2,4,32,128]{4,3,2,1,0:T(8,128)(2,1)S(1)}, bf16[2,2,4,32,128]{4,3,2,1,0:T(8,128)(2,1)S(1)}, u32[]{:S(2)}, u32[]{:S(2)}) collective-permute-start(bf16[2,2,4,32,128]{4,3,2,1,0:T(8,128)(2,1)S(1)} %get-tuple-element.18), channel_id=1, source_target_pairs={{0,6},{1,7},{2,4},{3,5},{4,2},{5,3},{6,0},{7,1},{8,14},{9,15},{10,... | collective-permute-start | bytes 393224 | tf_op jit(solution)/shard_map/ppermute | solution.py:335
  40.8 22.2 %copy-start.4 = (f32[12,2,128]{2,1,0:T(2,128)S(1)}, f32[12,2,128]{2,1,0:T(2,128)}, u32[]{:S(2)}) copy-start(f32[12,2,128]{2,1,0:T(2,128)} %tr_ref.4) | copy-start | bytes 36868
  40.8 22.2 %copy-start.6 = (s32[64,12]{0,1:T(8,128)S(1)}, s32[64,12]{0,1:T(8,128)}, u32[]{:S(2)}) copy-start(s32[64,12]{0,1:T(8,128)} %param.22) | copy-start | bytes 9220
  40.8 9.0 %collective-permute-start.5 = (bf16[4,2,4,32,128]{4,3,2,1,0:T(8,128)(2,1)S(1)}, bf16[4,2,4,32,128]{4,3,2,1,0:T(8,128)(2,1)S(1)}, u32[]{:S(2)}, u32[]{:S(2)}) collective-permute-start(bf16[4,2,4,32,128]{4,3,2,1,0:T(8,128)(2,1)S(1)} %shard_map.168), channel_id=1, source_target_pairs={{0,8},{1,9},{2,10},{3,11},{4,12},{5,13},{6,14},{7,15},{8,0},{9,1},... | collective-permute-start | bytes 786440 | tf_op jit(solution)/shard_map/ppermute | solution.py:335
  49.9 2.9 %collective-permute-start.6 = (bf16[2,4,4,32,128]{4,3,2,1,0:T(8,128)(2,1)S(1)}, bf16[2,4,4,32,128]{4,3,2,1,0:T(8,128)(2,1)S(1)}, u32[]{:S(2)}, u32[]{:S(2)}) collective-permute-start(bf16[2,4,4,32,128]{4,3,2,1,0:T(8,128)(2,1)S(1)} %shard_map.169), channel_id=1, source_target_pairs={{0,1},{1,0},{2,3},{3,2},{4,5},{5,4},{6,7},{7,6},{8,9},{9,8},{10,11... | collective-permute-start | bytes 786440 | tf_op jit(solution)/shard_map/ppermute | solution.py:335
  50.0 6.6 %collective-permute-start = (bf16[4,32,512]{2,1,0:T(8,128)(2,1)S(1)}, bf16[4,32,512]{2,1,0:T(8,128)(2,1)S(1)}, u32[]{:S(2)}, u32[]{:S(2)}) collective-permute-start(bf16[4,32,512]{2,1,0:T(8,128)(2,1)S(1)} %copy-done.8), channel_id=1, source_target_pairs={{0,1},{1,0},{2,3},{3,2},{4,5},{5,4},{6,7},{7,6},{8,9},{9,8},{10,11... | collective-permute-start | bytes 393224 | tf_op jit(solution)/shard_map/ppermute | solution.py:335
  50.5 10.2 %collective-permute-start.1 = (bf16[4,32,512]{2,1,0:T(8,128)(2,1)S(1)}, bf16[4,32,512]{2,1,0:T(8,128)(2,1)S(1)}, u32[]{:S(2)}, u32[]{:S(2)}) collective-permute-start(bf16[4,32,512]{2,1,0:T(8,128)(2,1)S(1)} %copy-done.7), channel_id=1, source_target_pairs={{1,2},{3,4},{5,6},{7,8},{9,10},{11,12},{13,14},{15,16},{17,18},{19... | collective-permute-start | bytes 393224 | tf_op jit(solution)/shard_map/ppermute | solution.py:343
  52.9 10.1 %collective-permute-start.7 = (bf16[4,32,128]{2,1,0:T(8,128)(2,1)S(1)}, bf16[4,32,128]{2,1,0:T(8,128)(2,1)S(1)}, u32[]{:S(2)}, u32[]{:S(2)}) collective-permute-start(bf16[4,32,128]{2,1,0:T(8,128)(2,1)S(1)} %get-tuple-element.20), channel_id=1, source_target_pairs={{0,16},{16,0},{32,48},{48,32},{64,80},{80,64},{96,112},{112,96},{1... | collective-permute-start | bytes 98312 | tf_op jit(solution)/shard_map/ppermute | solution.py:335
  55.1 7.9 %collective-permute-start.8 = (bf16[4,32,128]{2,1,0:T(8,128)(2,1)S(1)}, bf16[4,32,128]{2,1,0:T(8,128)(2,1)S(1)}, u32[]{:S(2)}, u32[]{:S(2)}) collective-permute-start(bf16[4,32,128]{2,1,0:T(8,128)(2,1)S(1)} %get-tuple-element.21), channel_id=1, source_target_pairs={{16,32},{48,64},{80,96},{112,128},{144,160},{176,192},{208,224},{3... | collective-permute-start | bytes 98312 | tf_op jit(solution)/shard_map/ppermute | solution.py:343

commit v4 on v3

v4 whole, which is shorter than its diff:
```python
import jax
import jax.numpy as jnp
from jax import lax
from jax.experimental import pallas as pl
from jax.experimental.pallas import tpu as pltpu
from jax.sharding import PartitionSpec as P


REACH = 7
HALO = 4
ALL = ("box", "dir")
F32 = jnp.float32
BF16 = jnp.bfloat16
OFFSETS = list(range(-REACH, -1)) + list(range(2, REACH + 1))
VMEM = pl.BlockSpec(memory_space=pltpu.VMEM)
ANY = pl.BlockSpec(memory_space=pl.ANY)
SMEM = pl.BlockSpec(memory_space=pltpu.SMEM)


def cos_sin(x):
    y = 0.5 * x
    z = y * y
    s = y * (
        1.0
        + z * (-1 / 6 + z * (1 / 120 + z * (-1 / 5040 + z * (1 / 362880 + z * (-1 / 39916800)))))
    )
    c = 1.0 + z * (
        -0.5
        + z * (1 / 24 + z * (-1 / 720 + z * (1 / 40320 + z * (-1 / 3628800 + z * (1 / 479001600)))))
    )
    return 1.0 - 2.0 * s * s, 2.0 * s * c


def iota(shape, dim):
    return lax.broadcasted_iota(jnp.int32, shape, dim)


def dot(a, b):
    return jnp.dot(a, b, preferred_element_type=F32)


def dot_nt(a, b):
    return lax.dot_general(a, b, (((1,), (1,)), ((), ())), preferred_element_type=F32)


def one_hot(cond):
    return cond.astype(F32).astype(BF16)


def slot_rows(slot_ref, first, count):
    row = iota((count, 128), 0)
    slot = jnp.zeros((count, 128), jnp.int32)
    for b in range(count):
        slot = jnp.where(row == b, slot_ref[first + b], slot)
    return slot


def child_cos_sin(part, slot):
    rows = jnp.broadcast_to(part[3:4, :], slot.shape)
    for j in range(3):
        rows = jnp.where(slot == j, part[j : j + 1, :], rows)
    return cos_sin(rows)


def middle_kernel(
    x_ref,
    theta_ref,
    phi_ref,
    phase_ref,
    slot_ref,
    out_ref,
    keep_ref,
    send_ref,
    ea_ref,
    eb_ref,
    m_ref,
    cs_ref,
    l_ref,
):
    boxes, parts, dirs = x_ref.shape
    t_n, t2_n = theta_ref.shape
    p_n, q_n = phi_ref.shape
    wide = t2_n * q_n
    step = 256
    repeat = one_hot(iota((q_n, step), 1) % q_n == iota((q_n, step), 0))
    phi_row = dot(phi_ref[...], repeat)
    slot = slot_rows(slot_ref, lax.axis_index("dir") * boxes, boxes)
    mine = lax.axis_index("dir")
    core = mine % 2
    ea_ref[...] = x_ref[pl.ds((1 - core) * (boxes - HALO), HALO)]
    eb_ref[...] = x_ref[pl.ds(core * (boxes - HALO), HALO)]
    x = x_ref[...].reshape(boxes * parts, dirs)
    half = parts // 2
    same = jnp.broadcast_to(core, (parts, 128)) == 0

    def prepare(e):
        n = lax.bitwise_xor(mine // 2, e)
        t2 = n * (step // q_n) + iota((t2_n, step), 1) // q_n
        theta_row = dot(theta_ref[...], one_hot(t2 == iota((t2_n, step), 0)))
        for t in range(t_n):
            m_ref[e % 2, t * p_n : (t + 1) * p_n, :] = (theta_row[t : t + 1, :] * phi_row).astype(BF16)
        for k in range(step // 128):
            start = pl.multiple_of(n * step + k * 128, 128)
            cos, sin = child_cos_sin(phase_ref[:, pl.ds(start, 128)], slot)
            cs_ref[e % 2, 0, :, k * 128 : (k + 1) * 128] = cos
            cs_ref[e % 2, 1, :, k * 128 : (k + 1) * 128] = sin

    prepare(0)
    for e in range(wide // step):
        n = lax.bitwise_xor(mine // 2, e)
        l_ref[e % 2] = dot(x, m_ref[e % 2])
        if e + 1 < wide // step:
            prepare(e + 1)
        for p in range(boxes // 4):
            re = jnp.zeros((half, step), F32)
            im = jnp.zeros((half, step), F32)
            for b in range(4 * p, 4 * p + 4):
                c = cs_ref[e % 2, 0, b : b + 1, :]
                s = cs_ref[e % 2, 1, b : b + 1, :]
                lr = l_ref[e % 2, b * parts : b * parts + half, :]
                li = l_ref[e % 2, b * parts + half : (b + 1) * parts, :]
                re = re + (c * lr - s * li)
                im = im + (c * li + s * lr)
            both = jnp.concatenate([re, im], axis=0)
            first = both[:, :128]
            second = both[:, 128:]
            out_ref[2 * n, p] = first.astype(BF16)
            out_ref[2 * n + 1, p] = second.astype(BF16)
            keep_ref[e, p] = jnp.where(same, first, second).astype(BF16)
            send_ref[e, p] = jnp.where(same, second, first).astype(BF16)


def coarse_kernel(
    par_ref, theta_ref, phi_ref, phase_ref, slot_ref, out_ref, a_ref, cs_ref, l_ref, v_ref
):
    blocks, kids, parts, lanes = par_ref.shape
    t_n, t2_n = theta_ref.shape
    p_n, q_n = phi_ref.shape
    pair = lanes // p_n
    tall = one_hot(iota((lanes, p_n), 0) % p_n == iota((lanes, p_n), 1))
    phi_tall = dot(tall, phi_ref[...])
    w = jnp.concatenate(
        [jnp.where(iota((lanes, q_n), 0) // p_n == h, phi_tall, 0.0) for h in range(pair)], axis=1
    ).astype(BF16)
    e1 = one_hot(iota((t2_n * 8, t2_n), 0) // 8 == iota((t2_n * 8, t2_n), 1))
    e2 = one_hot(iota((t_n, t_n * 8), 1) // 8 == iota((t_n, t_n * 8), 0))
    stretched = dot(dot_nt(e1, theta_ref[...]).astype(BF16), e2)
    same = iota(stretched.shape, 0) % 8 == iota(stretched.shape, 1) % 8
    k8 = jnp.where(same, stretched, 0.0).astype(BF16)
    rows = kids * parts
    slot = slot_rows(slot_ref, lax.axis_index("dir") * kids, kids)
    for d in range(blocks):
        a_ref[d] = dot(par_ref[d].reshape(rows, lanes), w)
        for t2 in range(d * t2_n // blocks, (d + 1) * t2_n // blocks):
            cols = slice(t2 * q_n, (t2 + 1) * q_n)
            cos, sin = child_cos_sin(phase_ref[:, cols], slot)
            cs_ref[0, :, cols] = cos
            cs_ref[1, :, cols] = sin

    def lift(m, a):
        cols = []
        for r in (m * parts + 8 * a, m * parts + 16 + 8 * a):
            pieces = [
                a_ref[t // pair, r : r + 8, (t % pair) * q_n : (t % pair + 1) * q_n]
                for t in range(t_n)
            ]
            cols.append(jnp.concatenate(pieces, axis=0).astype(BF16))
        l_ref[m, a] = dot(k8, jnp.concatenate(cols, axis=1))

    def combine(t2, a):
        cols = slice(t2 * q_n, (t2 + 1) * q_n)
        re = jnp.zeros((8, q_n), F32)
        im = jnp.zeros((8, q_n), F32)
        for m in range(kids):
            c = cs_ref[0, m : m + 1, cols]
            s = cs_ref[1, m : m + 1, cols]
            lr = l_ref[m, a, t2 * 8 : t2 * 8 + 8, :q_n]
            li = l_ref[m, a, t2 * 8 : t2 * 8 + 8, q_n:]
            re = re + (c * lr - s * li)
            im = im + (c * li + s * lr)
        return re, im

    for m in range(kids):
        lift(m, 0)
    for m in range(kids):
        lift(m, 1)
        for t2 in range(m * t2_n // kids, (m + 1) * t2_n // kids):
            v_ref[t2, 0], v_ref[t2, 1] = combine(t2, 0)
    lane = iota((8, q_n), 1)
    low = lane < 64
    even = lane % 64 < 32
    for t2 in range(t2_n):
        v = {(0, 0): v_ref[t2, 0], (1, 0): v_ref[t2, 1]}
        v[0, 1], v[1, 1] = combine(t2, 1)
        u = {}
        for a in range(2):
            u[0, a] = jnp.where(low, v[0, a], pltpu.roll(v[1, a], 64, 1))
            u[1, a] = jnp.where(low, pltpu.roll(v[0, a], 64, 1), v[1, a])
        for h in range(2):
            out_ref[t2 * 4 + 2 * h] = jnp.where(even, u[h, 0], pltpu.roll(u[h, 1], 32, 1)).astype(BF16)
            out_ref[t2 * 4 + 2 * h + 1] = jnp.where(
                even, pltpu.roll(u[h, 0], 96, 1), u[h, 1]
            ).astype(BF16)


def pack_x_kernel(own_ref, other_ref, out_ref):
    for core, ref in enumerate((own_ref, other_ref)):
        out_ref[core] = ref[4:]


def pack_y_kernel(own_ref, other_ref, x_ref, *out_refs):
    for y, ref in enumerate(out_refs):
        ref[0, 0] = own_ref[y + 1]
        ref[0, 1] = other_ref[y + 1]
        ref[1, 0] = x_ref[0, y + 1]
        ref[1, 1] = x_ref[1, y + 1]


def gather_kernel(
    own_ref, other_ref, x_ref, y1_ref, y2_ref, y3_ref, out_ref, ea_ref, eb_ref
):
    mine = lax.axis_index("dir")
    out_ref[mine] = own_ref[0]
    out_ref[lax.bitwise_xor(mine, 1)] = other_ref[0]
    out_ref[lax.bitwise_xor(mine, 8)] = x_ref[0, 0]
    out_ref[lax.bitwise_xor(mine, 9)] = x_ref[1, 0]
    for y, ref in enumerate((y1_ref, y2_ref, y3_ref)):
        for x in range(2):
            for core in range(2):
                out_ref[lax.bitwise_xor(mine, 8 * x + 2 * (y + 1) + core)] = ref[x, core]
    last = out_ref.shape[0] - 1
    odd = lax.axis_index("box") % 2
    ea_ref[...] = out_ref[(1 - odd) * last]
    eb_ref[...] = out_ref[odd * last]


def codes_by_lane(list_ref, first):
    entry = list_ref[...]
    place = entry - (first + iota(entry.shape, 1)) + REACH
    bits = jnp.where(entry >= 0, lax.shift_left(jnp.ones_like(entry), jnp.maximum(place, 0)), 0)
    row = jnp.sum(bits.astype(F32), axis=0, keepdims=True)
    return jnp.transpose(jnp.broadcast_to(row, (8, row.shape[1])))[:, :1].astype(jnp.int32)


def codes_by_row(list_ref, first):
    entry = list_ref[...]
    place = entry - (first + iota(entry.shape, 0)) + REACH
    bits = jnp.where(entry >= 0, lax.shift_left(jnp.ones_like(entry), jnp.maximum(place, 0)), 0)
    return jnp.sum(bits.astype(F32), axis=1, keepdims=True).astype(jnp.int32)


def masked(code, offset):
    return lax.bitwise_and(code, 1 << (offset + REACH)) != 0


def group_offsets(r):
    return [o for o in OFFSETS if -HALO <= r + o < 2 * HALO]


def fill_masks(mt_ref, tr_ref, code):
    boxes, dirs = mt_ref.shape[2:]
    code = jnp.broadcast_to(code, (boxes, 128))
    for k in range(dirs // 128):
        cols = slice(k * 128, (k + 1) * 128)
        for slot, o in enumerate(OFFSETS):
            here = masked(code, o)
            mt_ref[slot, 0, :, cols] = jnp.where(here, tr_ref[slot, 0:1, cols], 0.0)
            mt_ref[slot, 1, :, cols] = jnp.where(here, tr_ref[slot, 1:2, cols], 0.0)


def translate_groups(f_ref, mt_ref, out_ref, groups, start):
    half, dirs = f_ref.shape[1] // 2, f_ref.shape[2]
    for k in range(dirs // 128):
        cols = slice(k * 128, (k + 1) * 128)
        for i in [4 * g + r for g in groups for r in range(4)]:
            re = jnp.zeros((half, 128), F32)
            im = jnp.zeros((half, 128), F32)
            for o in group_offsets(i % 4):
                slot = OFFSETS.index(o)
                a = mt_ref[slot, 0, i : i + 1, cols]
                b = mt_ref[slot, 1, i : i + 1, cols]
                xr = f_ref[i + HALO + o, :half, cols]
                xi = f_ref[i + HALO + o, half:, cols]
                re = re + (a * xr - b * xi)
                im = im + (a * xi + b * xr)
            out_ref[i - start, :, cols] = jnp.concatenate([re, im], axis=0).astype(BF16)


def place_edges(f_ref, a_ref, b_ref, odd):
    far = f_ref.shape[0] - HALO
    f_ref[pl.ds((1 - odd) * far, HALO)] = a_ref[...].astype(F32)
    f_ref[pl.ds(odd * far, HALO)] = b_ref[...].astype(F32)


def fine_inner_kernel(x_any, list_ref, tr_ref, inner_ref, copy_ref, mt_ref, sem, f_ref):
    fetch = pltpu.make_async_copy(x_any, copy_ref, sem)
    fetch.start()
    boxes = copy_ref.shape[0]
    first = lax.axis_index("box") * lax.axis_size("dir") + lax.axis_index("dir")
    fill_masks(mt_ref, tr_ref, codes_by_row(list_ref, first * boxes))
    fetch.wait()
    f_ref[HALO : HALO + boxes] = copy_ref[...].astype(F32)
    translate_groups(f_ref, mt_ref, inner_ref, range(1, boxes // 4 - 1), 4)


def fine_outer_kernel(inner_ref, x_ref, mt_ref, a_ref, b_ref, out_ref, f_ref):
    boxes = x_ref.shape[0]
    place_edges(f_ref, a_ref, b_ref, lax.axis_index("dir") % 2)
    f_ref[HALO : HALO + boxes] = x_ref[...].astype(F32)
    out_ref[4 : boxes - 4] = inner_ref[...]
    translate_groups(f_ref, mt_ref, out_ref, (0, boxes // 4 - 1), 0)


def middle_masks_kernel(list_ref, tr_ref, mt_ref):
    boxes = mt_ref.shape[2]
    fill_masks(mt_ref, tr_ref, codes_by_lane(list_ref, lax.axis_index("box") * boxes))


def middle_translate_kernel(x_ref, a_ref, b_ref, mt_ref, out_ref, f_ref):
    boxes = x_ref.shape[0]
    place_edges(f_ref, a_ref, b_ref, lax.axis_index("box") % 2)
    f_ref[HALO : HALO + boxes] = x_ref[...].astype(F32)
    translate_groups(f_ref, mt_ref, out_ref, range(boxes // 4), 0)


def coarse_masks_kernel(list_ref, tr_ref, out_ref):
    boxes = out_ref.shape[2]
    code = jnp.broadcast_to(codes_by_lane(list_ref, 0), (boxes, 128))
    low = iota((1, 128), 1) < 64
    for slot, o in enumerate(OFFSETS):
        here = masked(code, o)
        a = jnp.concatenate([tr_ref[slot, 0:1, :]] * 4, axis=1)
        b = jnp.concatenate([tr_ref[slot, 1:2, :]] * 4, axis=1)
        b = jnp.where(low, -b, b)
        out_ref[slot, 0] = jnp.where(here, a, 0.0)
        out_ref[slot, 1] = jnp.where(here, b, 0.0)


def coarse_translate_kernel(
    x_any, mt_ref, out_any, x_ref, o_ref, in_sem, out_sem, f_ref, r_ref, y_ref
):
    boxes, sub, lanes = x_ref.shape
    chunks = in_sem.shape[0]
    size = boxes // chunks
    fetches = []
    for q in range(chunks):
        part = pl.ds(q * size, size)
        fetches.append(pltpu.make_async_copy(x_any.at[part], x_ref.at[part], in_sem.at[q]))
        fetches[q].start()
    zero = jnp.zeros((HALO, sub, lanes), F32)
    for ref in (f_ref, r_ref):
        ref[:HALO] = zero
        ref[HALO + boxes :] = zero

    def group(g):
        for r in range(4):
            i = 4 * g + r
            acc = jnp.zeros((sub, lanes), F32)
            for o in group_offsets(r):
                slot = OFFSETS.index(o)
                a = mt_ref[slot, 0, i : i + 1, :]
                b = mt_ref[slot, 1, i : i + 1, :]
                acc = acc + (a * f_ref[i + HALO + o] + b * r_ref[i + HALO + o])
            y_ref[i * sub : (i + 1) * sub, :] = acc

    stores = []

    def finish(h):
        for s in range(sub):
            turned = jnp.transpose(y_ref[pl.ds(h * lanes * sub + s, lanes, stride=sub), :])
            for cb in range(4):
                o_ref[h, 8 * cb + s] = turned[32 * cb : 32 * cb + 32, :].astype(BF16)
        target = out_any.at[:, :, pl.ds(h * lanes, lanes)]
        stores.append(pltpu.make_async_copy(o_ref.at[h], target, out_sem.at[h]))
        stores[h].start()

    done = 0
    for q in range(chunks):
        fetches[q].wait()
        x = x_ref[q * size : (q + 1) * size].astype(F32)
        here = slice(HALO + q * size, HALO + (q + 1) * size)
        f_ref[here] = x
        r_ref[here] = pltpu.roll(x.reshape(size * sub, lanes), 64, 1).reshape(x.shape)
        upto = boxes // 4 if q + 1 == chunks else (q + 1) * size // 4 - 1
        for g in range(done, upto):
            group(g)
            if (4 * g + 4) % lanes == 0:
                finish((4 * g + 4) // lanes - 1)
        done = upto
    for copy in stores:
        copy.wait()


def near(x):
    return pltpu.with_memory_space_constraint(x, pltpu.VMEM)


def call(body, out, specs, scratch, *args, limit=24 << 20, out_space=VMEM):
    return pl.pallas_call(
        body,
        out_shape=out,
        in_specs=specs,
        out_specs=jax.tree.map(lambda _: out_space, out),
        scratch_shapes=scratch,
        compiler_params=pltpu.CompilerParams(vmem_limit_bytes=limit),
    )(*args)


def swap(x, axis, bits):
    return lax.ppermute(x, axis, [(i, i ^ bits) for i in range(lax.axis_size(axis))])


def halo(first, second, axes):
    count = lax.axis_size(axes)
    pairs = [(i, i + 1) for i in range(1, count - 1, 2)]
    pairs = pairs + [(b, a) for a, b in pairs]
    a = swap(first, axes, 1)
    return a, lax.ppermute(second, axes, pairs)


def local(
    fine_out,
    fine_list,
    fine_slot,
    fine_translator,
    theta_up_fine,
    phi_up_fine,
    middle_phase,
    middle_list,
    middle_slot,
    middle_translator,
    theta_up_middle,
    phi_up_middle,
    coarse_phase,
    coarse_list,
    coarse_translator,
):
    shape = jax.ShapeDtypeStruct
    boxes, parts, dirs = fine_out.shape
    dir_n = lax.axis_size("dir")
    all_n = dir_n * lax.axis_size("box")
    wide = middle_phase.shape[1]
    widest = coarse_phase.shape[1]
    kids = boxes // 4
    width = wide // dir_n
    piece = (kids, parts, width)
    edge = shape((HALO, parts, dirs), BF16)
    parents, own, other, fine_a, fine_b = call(
        middle_kernel,
        (pltpu.VMEM((dir_n,) + piece, BF16),)
        + (pltpu.VMEM((dir_n // 2,) + piece, BF16),) * 2
        + (edge, edge),
        [VMEM] * 4 + [SMEM],
        [
            pltpu.VMEM((2, dirs, 256), BF16),
            pltpu.VMEM((2, 2, boxes, 256), F32),
            pltpu.VMEM((2, boxes * parts, 256), F32),
        ],
        fine_out,
        theta_up_fine.T,
        phi_up_fine.T,
        middle_phase,
        fine_slot,
        limit=60 * 1024 * 1024,
    )
    own = near(own)
    other = near(swap(other, "dir", 1))
    xs = pltpu.VMEM((2, dir_n // 4) + piece, BF16)
    xs = call(pack_x_kernel, xs, [VMEM] * 2, [], own, other)
    xs = near(swap(xs, "dir", 8))
    t2_n = theta_up_middle.shape[0]
    q_n = phi_up_middle.shape[0]
    chunks = call(coarse_kernel,
        pltpu.VMEM((all_n, 8, 128), BF16),
        [VMEM] * 4 + [SMEM],
        [
            pltpu.VMEM((dir_n, kids * parts, 2 * q_n), F32),
            pltpu.VMEM((2, kids, widest), F32),
            pltpu.VMEM((kids, 2, t2_n * 8, 2 * q_n), F32),
            pltpu.VMEM((t2_n, 2, 8, q_n), F32),
        ],
        near(parents),
        theta_up_middle.T,
        phi_up_middle.T,
        coarse_phase,
        middle_slot,
        limit=60 * 1024 * 1024,
    )
    coarse_held = lax.all_to_all(chunks, ALL, split_axis=0, concat_axis=0, tiled=True)
    ys = (pltpu.VMEM((2, 2) + piece, BF16),) * 3
    ys = call(pack_y_kernel, ys, [VMEM] * 3, [], own, other, xs)
    ys = tuple(near(swap(y, "dir", bits)) for y, bits in zip(ys, (2, 4, 6)))
    edge = shape(piece, BF16)
    middle_out, middle_a, middle_b = call(
        gather_kernel,
        (pltpu.VMEM((dir_n,) + piece, BF16), edge, edge),
        [VMEM] * 6,
        [],
        own,
        other,
        xs,
        *ys,
    )
    middle_out = middle_out.reshape(dir_n * kids, parts, width)
    fine_a, fine_b = halo(fine_a, fine_b, ALL)
    inner, fine_copy, fine_masks = call(
        fine_inner_kernel,
        (
            pltpu.VMEM((boxes - 8, parts, dirs), BF16),
            pltpu.VMEM(fine_out.shape, BF16),
            pltpu.VMEM((12, 2, boxes, dirs), F32),
        ),
        [ANY] + [VMEM] * 2,
        [pltpu.SemaphoreType.DMA(()), pltpu.VMEM((boxes + 2 * HALO, parts, dirs), F32)],
        pltpu.with_memory_space_constraint(fine_out, pltpu.HBM),
        fine_list,
        fine_translator,
    )
    fine_in = call(
        fine_outer_kernel,
        shape(fine_out.shape, BF16),
        [VMEM] * 5,
        [pltpu.VMEM((boxes + 2 * HALO, parts, dirs), F32)],
        near(inner),
        near(fine_copy),
        near(fine_masks),
        near(fine_a),
        near(fine_b),
    )
    masks = call(
        coarse_masks_kernel,
        pltpu.VMEM((12, 2, all_n, 128), F32),
        [VMEM] * 2,
        [],
        coarse_list.T,
        coarse_translator,
    )
    middle_a, middle_b = halo(middle_a, middle_b, "box")
    held, _, lanes = middle_out.shape
    middle_masks = call(
        middle_masks_kernel,
        pltpu.VMEM((12, 2, held, lanes), F32),
        [VMEM] * 2,
        [],
        middle_list.T,
        middle_translator,
    )
    middle_in = call(
        middle_translate_kernel,
        shape(middle_out.shape, BF16),
        [VMEM] * 4,
        [pltpu.VMEM((held + 2 * HALO, parts, lanes), F32)],
        near(middle_out),
        near(middle_a),
        near(middle_b),
        near(middle_masks),
    )
    coarse_in = call(
        coarse_translate_kernel,
        shape((parts, widest // all_n, all_n), BF16),
        [ANY, VMEM],
        [
            pltpu.VMEM((all_n, 8, 128), BF16),
            pltpu.VMEM((all_n // 128, parts, widest // all_n, 128), BF16),
            pltpu.SemaphoreType.DMA((4,)),
            pltpu.SemaphoreType.DMA((all_n // 128,)),
            pltpu.VMEM((all_n + 2 * HALO, 8, 128), F32),
            pltpu.VMEM((all_n + 2 * HALO, 8, 128), F32),
            pltpu.VMEM((all_n * 8, 128), F32),
        ],
        coarse_held,
        near(masks),
        out_space=ANY,
    )
    return fine_in, middle_in, jnp.transpose(coarse_in, (2, 0, 1))


def solution(mesh):
    return jax.shard_map(
        local,
        mesh=mesh,
        in_specs=(
            P(ALL, None, None),
            P(ALL, None),
            P("box"),
            P(),
            P(),
            P(),
            P(),
            P("box", None),
            P("box"),
            P(None, None, "dir"),
            P(),
            P(),
            P(),
            P(),
            P(None, None, ALL),
        ),
        out_specs=(P(ALL, None, None), P("box", None, "dir"), P(None, None, ALL)),
        check_vma=False,
    )
```

time: 69.1 us -> 68.2 us (0.987)
  the two profiles are of different devices: /device:TPU:4 before, /device:TPU:34 now
where the time goes in v4:
time: 68.2 us; the launch traced here: 68 us
  starting transfers between devices  33.6 us (49%)
  Pallas kernels  17.6 us (26%)
  waiting for transfers between devices  15.7 us (23%)
  between operations  0.98 us (1%)
    pallas_call x11, Pallas kernels, call(): pl.pallas_call(body, out_shape=out, in_specs=specs, out_specs=jax.tree.ma...  17.6 us
    ppermute x7, waiting for transfers between devices, swap(): lax.ppermute(x, axis, [(i, i ^ bits) for i in range(lax.axis_size(axis))])  15.7 us
    all_to_all x1, starting transfers between devices, local(): lax.all_to_all(chunks, ALL, split_axis=0, concat_axis=0, tiled=True)  15.4 us
    ppermute x2, starting transfers between devices, halo(): return (a, lax.ppermute(second, axes, pairs))  11 us
    ppermute x7, starting transfers between devices, swap(): lax.ppermute(x, axis, [(i, i ^ bits) for i in range(lax.axis_size(axis))])  7.28 us
  transfers between devices with their start and end apart: 10, of which 4 were waited for; matrix products, arithmetic and copies ran while one was open for 0% of the time, Pallas kernels for 9%

profile of v4, /device:TPU:34, one launch (start us, length us, event | category | flops | bytes accessed | tf_op | source)
XLA Modules:
  0.0 68.0 jit_solution(8162821810595507427)
XLA Ops:
  0.7 3.9 %shard_map.167 = (bf16[16,4,32,128]{3,2,1,0:T(8,128)(2,1)S(1)}, bf16[8,4,32,128]{3,2,1,0:T(8,128)(2,1)S(1)}, bf16[8,4,32,128]{3,2,1,0:T(8,128)(2,1)S(1)}, bf16[4,32,512]{2,1,0:T(8,128)(2,1)}, bf16[4,32,512]{2,1,0:T(8,128)(2,1)}) custom-call(bf16[16,32,512]{2,1,0:T(8,128)(2,1)} %x_ref.1, bf16[16,32]{1,0:T(8,128)(2,1)} %bitcast.15, bf16[32,64]{1,0:T(8,128)(2,1)} %bitcast.13, ...), custom_call_target="tpu_custom_call" | custom-call | tf_op jit(solution)/shard_map/pallas_call | solution.py:399
  4.5 0.0 copy-start.2
  4.6 3.8 %shard_map.174 = bf16[256,8,128]{2,1,0:T(8,128)(2,1)} custom-call(bf16[16,4,32,128]{3,2,1,0:T(8,128)(2,1)S(1)} %get-tuple-element.30.par_ref, bf16[32,64]{1,0:T(8,128)(2,1)} %bitcast.14, bf16[64,128]{1,0:T(8,128)(2,1)} %bitcast.12, f32[4,8192]{1,0:T(4,128)} %phase_ref.3, s32[64]{0:T(128)} %slot_ref.3), custom_call_target="tpu_custom_call" | custom-call | tf_op jit(solution)/shard_map/pallas_call | solution.py:399
  8.3 15.4 %all-to-all-start = ((bf16[256,8,128]{2,1,0:T(8,128)(2,1)}), bf16[256,8,128]{2,1,0:T(8,128)(2,1)}, u32[]{:S(2)}, u32[]{:S(2)}) async-start(bf16[256,8,128]{2,1,0:T(8,128)(2,1)} %shard_map.174), calls=%async_computation | async-start | bytes 1048576 | tf_op jit(solution)/shard_map/all_to_all | solution.py:489
  23.7 0.2 collective-permute-start.2
  23.9 1.4 %collective-permute-done.2.other_ref = bf16[8,4,32,128]{3,2,1,0:T(8,128)(2,1)S(1)} collective-permute-done((bf16[8,4,32,128]{3,2,1,0:T(8,128)(2,1)S(1)}, bf16[8,4,32,128]{3,2,1,0:T(8,128)(2,1)S(1)}, u32[]{:S(2)}, u32[]{:S(2)}) %collective-permute-start.2) | collective-permute-done | bytes 262176 | tf_op jit(solution)/shard_map/ppermute | solution.py:410
  25.3 2.2 %collective-permute-start.3 = (bf16[2,4,4,32,128]{4,3,2,1,0:T(8,128)(2,1)S(1)}, bf16[2,4,4,32,128]{4,3,2,1,0:T(8,128)(2,1)S(1)}, u32[]{:S(2)}, u32[]{:S(2)}) collective-permute-start(bf16[2,4,4,32,128]{4,3,2,1,0:T(8,128)(2,1)S(1)} %shard_map.169), channel_id=1, source_target_pairs={{0,8},{1,9},{2,10},{3,11},{4,12},{5,13},{6,14},{7,15},{8,0},{9,1},... | collective-permute-start | bytes 786440 | tf_op jit(solution)/shard_map/ppermute | solution.py:410
  27.5 10.7 %collective-permute-done.3.x_ref = bf16[2,4,4,32,128]{4,3,2,1,0:T(8,128)(2,1)S(1)} collective-permute-done((bf16[2,4,4,32,128]{4,3,2,1,0:T(8,128)(2,1)S(1)}, bf16[2,4,4,32,128]{4,3,2,1,0:T(8,128)(2,1)S(1)}, u32[]{:S(2)}, u32[]{:S(2)}) %collective-permute-start.3) | collective-permute-done | bytes 262176 | tf_op jit(solution)/shard_map/ppermute | solution.py:410
  38.3 1.6 %collective-permute-start.4 = (bf16[2,2,4,32,128]{4,3,2,1,0:T(8,128)(2,1)S(1)}, bf16[2,2,4,32,128]{4,3,2,1,0:T(8,128)(2,1)S(1)}, u32[]{:S(2)}, u32[]{:S(2)}) collective-permute-start(bf16[2,2,4,32,128]{4,3,2,1,0:T(8,128)(2,1)S(1)} %get-tuple-element.24), channel_id=1, source_target_pairs={{0,2},{1,3},{2,0},{3,1},{4,6},{5,7},{6,4},{7,5},{8,10},{9,11},{10,... | collective-permute-start | bytes 393224 | tf_op jit(solution)/shard_map/ppermute | solution.py:410
  39.9 2.9 %collective-permute-start.5 = (bf16[2,2,4,32,128]{4,3,2,1,0:T(8,128)(2,1)S(1)}, bf16[2,2,4,32,128]{4,3,2,1,0:T(8,128)(2,1)S(1)}, u32[]{:S(2)}, u32[]{:S(2)}) collective-permute-start(bf16[2,2,4,32,128]{4,3,2,1,0:T(8,128)(2,1)S(1)} %get-tuple-element.25), channel_id=1, source_target_pairs={{0,4},{1,5},{2,6},{3,7},{4,0},{5,1},{6,2},{7,3},{8,12},{9,13},{10,... | collective-permute-start | bytes 393224 | tf_op jit(solution)/shard_map/ppermute | solution.py:410
  42.8 0.3 collective-permute-start.6
  43.0 0.0 collective-permute-start
  43.1 5.3 %collective-permute-start.1 = (bf16[4,32,512]{2,1,0:T(8,128)(2,1)S(1)}, bf16[4,32,512]{2,1,0:T(8,128)(2,1)S(1)}, u32[]{:S(2)}, u32[]{:S(2)}) collective-permute-start(bf16[4,32,512]{2,1,0:T(8,128)(2,1)S(1)} %copy-done.6), channel_id=1, source_target_pairs={{1,2},{3,4},{5,6},{7,8},{9,10},{11,12},{13,14},{15,16},{17,18},{19... | collective-permute-start | bytes 393224 | tf_op jit(solution)/shard_map/ppermute | solution.py:418
  48.3 0.0 collective-permute-done.4.y1_ref
  48.4 0.2 collective-permute-done.5.y2_ref
  48.6 3.3 %collective-permute-done.6.y3_ref = bf16[2,2,4,32,128]{4,3,2,1,0:T(8,128)(2,1)S(1)} collective-permute-done((bf16[2,2,4,32,128]{4,3,2,1,0:T(8,128)(2,1)S(1)}, bf16[2,2,4,32,128]{4,3,2,1,0:T(8,128)(2,1)S(1)}, u32[]{:S(2)}, u32[]{:S(2)}) %collective-permute-start.6) | collective-permute-done | bytes 131104 | tf_op jit(solution)/shard_map/ppermute | solution.py:410
  51.9 0.1 shard_map.171
  51.9 0.1 collective-permute-start.7
  52.0 5.7 %collective-permute-start.8 = (bf16[4,32,128]{2,1,0:T(8,128)(2,1)S(1)}, bf16[4,32,128]{2,1,0:T(8,128)(2,1)S(1)}, u32[]{:S(2)}, u32[]{:S(2)}) collective-permute-start(bf16[4,32,128]{2,1,0:T(8,128)(2,1)S(1)} %get-tuple-element.29), channel_id=1, source_target_pairs={{16,32},{48,64},{80,96},{112,128},{144,160},{176,192},{208,224},{3... | collective-permute-start | bytes 98312 | tf_op jit(solution)/shard_map/ppermute | solution.py:418
  57.8 0.0 copy-done.3
  57.8 0.0 copy-done.4
  57.8 0.2 shard_map.172.mt_ref
  58.0 1.8 %shard_map.166 = (bf16[8,32,512]{2,1,0:T(8,128)(2,1)S(1)}, bf16[16,32,512]{2,1,0:T(8,128)(2,1)S(1)}, f32[12,2,16,512]{3,2,1,0:T(8,128)S(1)}) custom-call(bf16[16,32,512]{2,1,0:T(8,128)(2,1)} %x_ref.1, s32[16,12]{1,0:T(8,128)S(1)} %copy-done.5, f32[12,2,512]{2,1,0:T(2,128)S(1)} %copy-done), custom_call_target="tpu_custom_call" | custom-call | tf_op jit(solution)/shard_map/pallas_call | solution.py:399
  59.9 0.6 shard_map.175.mt_ref
  60.5 0.0 collective-permute-done.a_ref
  60.5 0.0 collective-permute-done.1.b_ref
  60.5 1.6 %shard_map.168 = bf16[16,32,512]{2,1,0:T(8,128)(2,1)} custom-call(bf16[8,32,512]{2,1,0:T(8,128)(2,1)S(1)} %get-tuple-element.17.inner_ref, bf16[16,32,512]{2,1,0:T(8,128)(2,1)S(1)} %get-tuple-element.18.x_ref, f32[12,2,16,512]{3,2,1,0:T(8,128)S(1)} %get-tuple-element.19.mt_ref, bf16[4,32,512]{2,1,0:T(8,128)(2,1)S(1)} %collective-permute-done.a_ref, ...), custom_call_target="tpu_custom_call" | custom-call | tf_op jit(solution)/shard_map/pallas_call | solution.py:399
  62.1 0.0 collective-permute-done.7.a_ref
  62.1 0.0 collective-permute-done.8.b_ref
  62.1 2.1 %shard_map.173 = bf16[64,32,128]{2,1,0:T(8,128)(2,1)} custom-call(bf16[64,32,128]{2,1,0:T(8,128)(2,1)S(1)} %bitcast.8, bf16[4,32,128]{2,1,0:T(8,128)(2,1)S(1)} %collective-permute-done.7.a_ref, bf16[4,32,128]{2,1,0:T(8,128)(2,1)S(1)} %collective-permute-done.8.b_ref, f32[12,2,64,128]{3,2,1,0:T(8,128)S(1)} %shard_map.172.mt_ref), custom_call_target="tpu_custom_call" | custom-call | tf_op jit(solution)/shard_map/pallas_call | solution.py:399
  64.2 0.0 all-to-all-done.x_any
  64.2 3.6 %shard_map.176 = bf16[32,32,256]{2,1,0:T(8,128)(2,1)} custom-call(bf16[256,8,128]{2,1,0:T(8,128)(2,1)} %all-to-all-done.x_any, f32[12,2,256,128]{3,2,1,0:T(8,128)S(1)} %shard_map.175.mt_ref), custom_call_target="tpu_custom_call" | custom-call | tf_op jit(solution)/shard_map/pallas_call | solution.py:399
  (15 shorter events, 0.1 us)
Async XLA Ops:
  0.6 57.1 %copy-start.3 = (f32[12,2,128]{2,1,0:T(2,128)S(1)}, f32[12,2,128]{2,1,0:T(2,128)}, u32[]{:S(2)}) copy-start(f32[12,2,128]{2,1,0:T(2,128)} %tr_ref.4) | copy-start | bytes 36868
  0.6 57.1 %copy-start.4 = (s32[64,12]{0,1:T(8,128)S(1)}, s32[64,12]{0,1:T(8,128)}, u32[]{:S(2)}) copy-start(s32[64,12]{0,1:T(8,128)} %param.22) | copy-start | bytes 9220
  0.7 57.4 %copy-start = (f32[12,2,512]{2,1,0:T(2,128)S(1)}, f32[12,2,512]{2,1,0:T(2,128)}, u32[]{:S(2)}) copy-start(f32[12,2,512]{2,1,0:T(2,128)} %tr_ref.3) | copy-start | bytes 147460
  0.7 57.4 %copy-start.5 = (s32[16,12]{1,0:T(8,128)S(1)}, s32[16,12]{1,0:T(8,128)}, u32[]{:S(2)}) copy-start(s32[16,12]{1,0:T(8,128)} %list_ref.1) | copy-start | bytes 2308
  4.5 38.5 %copy-start.7 = (bf16[4,32,512]{2,1,0:T(8,128)(2,1)S(1)}, bf16[4,32,512]{2,1,0:T(8,128)(2,1)}, u32[]{:S(2)}) copy-start(bf16[4,32,512]{2,1,0:T(8,128)(2,1)} %get-tuple-element.20) | copy-start | bytes 393220
  4.5 38.5 %copy-start.6 = (bf16[4,32,512]{2,1,0:T(8,128)(2,1)S(1)}, bf16[4,32,512]{2,1,0:T(8,128)(2,1)}, u32[]{:S(2)}) copy-start(bf16[4,32,512]{2,1,0:T(8,128)(2,1)} %get-tuple-element.21) | copy-start | bytes 393220
  4.5 55.3 %copy-start.1 = (s32[256,12]{0,1:T(8,128)S(1)}, s32[256,12]{0,1:T(8,128)}, u32[]{:S(2)}) copy-start(s32[256,12]{0,1:T(8,128)} %param.28) | copy-start | bytes 36868
  4.5 55.3 %copy-start.2 = (f32[12,2,32]{2,1,0:T(2,128)S(1)}, f32[12,2,32]{2,1,0:T(2,128)}, u32[]{:S(2)}) copy-start(f32[12,2,32]{2,1,0:T(2,128)} %tr_ref.5) | copy-start | bytes 9220
  8.3 55.9 %all-to-all-start = ((bf16[256,8,128]{2,1,0:T(8,128)(2,1)}), bf16[256,8,128]{2,1,0:T(8,128)(2,1)}, u32[]{:S(2)}, u32[]{:S(2)}) async-start(bf16[256,8,128]{2,1,0:T(8,128)(2,1)} %shard_map.174), calls=%async_computation | async-start | bytes 1048576 | tf_op jit(solution)/shard_map/all_to_all | solution.py:489
  23.7 1.6 %collective-permute-start.2 = (bf16[8,4,32,128]{3,2,1,0:T(8,128)(2,1)S(1)}, bf16[8,4,32,128]{3,2,1,0:T(8,128)(2,1)S(1)}, u32[]{:S(2)}, u32[]{:S(2)}) collective-permute-start(bf16[8,4,32,128]{3,2,1,0:T(8,128)(2,1)S(1)} %get-tuple-element.23), channel_id=1, source_target_pairs={{0,1},{1,0},{2,3},{3,2},{4,5},{5,4},{6,7},{7,6},{8,9},{9,8},{10,11... | collective-permute-start | bytes 786440 | tf_op jit(solution)/shard_map/ppermute | solution.py:410
  25.3 12.9 %collective-permute-start.3 = (bf16[2,4,4,32,128]{4,3,2,1,0:T(8,128)(2,1)S(1)}, bf16[2,4,4,32,128]{4,3,2,1,0:T(8,128)(2,1)S(1)}, u32[]{:S(2)}, u32[]{:S(2)}) collective-permute-start(bf16[2,4,4,32,128]{4,3,2,1,0:T(8,128)(2,1)S(1)} %shard_map.169), channel_id=1, source_target_pairs={{0,8},{1,9},{2,10},{3,11},{4,12},{5,13},{6,14},{7,15},{8,0},{9,1},... | collective-permute-start | bytes 786440 | tf_op jit(solution)/shard_map/ppermute | solution.py:410
  38.3 10.1 %collective-permute-start.4 = (bf16[2,2,4,32,128]{4,3,2,1,0:T(8,128)(2,1)S(1)}, bf16[2,2,4,32,128]{4,3,2,1,0:T(8,128)(2,1)S(1)}, u32[]{:S(2)}, u32[]{:S(2)}) collective-permute-start(bf16[2,2,4,32,128]{4,3,2,1,0:T(8,128)(2,1)S(1)} %get-tuple-element.24), channel_id=1, source_target_pairs={{0,2},{1,3},{2,0},{3,1},{4,6},{5,7},{6,4},{7,5},{8,10},{9,11},{10,... | collective-permute-start | bytes 393224 | tf_op jit(solution)/shard_map/ppermute | solution.py:410
  39.9 8.7 %collective-permute-start.5 = (bf16[2,2,4,32,128]{4,3,2,1,0:T(8,128)(2,1)S(1)}, bf16[2,2,4,32,128]{4,3,2,1,0:T(8,128)(2,1)S(1)}, u32[]{:S(2)}, u32[]{:S(2)}) collective-permute-start(bf16[2,2,4,32,128]{4,3,2,1,0:T(8,128)(2,1)S(1)} %get-tuple-element.25), channel_id=1, source_target_pairs={{0,4},{1,5},{2,6},{3,7},{4,0},{5,1},{6,2},{7,3},{8,12},{9,13},{10,... | collective-permute-start | bytes 393224 | tf_op jit(solution)/shard_map/ppermute | solution.py:410
  42.8 9.1 %collective-permute-start.6 = (bf16[2,2,4,32,128]{4,3,2,1,0:T(8,128)(2,1)S(1)}, bf16[2,2,4,32,128]{4,3,2,1,0:T(8,128)(2,1)S(1)}, u32[]{:S(2)}, u32[]{:S(2)}) collective-permute-start(bf16[2,2,4,32,128]{4,3,2,1,0:T(8,128)(2,1)S(1)} %get-tuple-element.26), channel_id=1, source_target_pairs={{0,6},{1,7},{2,4},{3,5},{4,2},{5,3},{6,0},{7,1},{8,14},{9,15},{10,... | collective-permute-start | bytes 393224 | tf_op jit(solution)/shard_map/ppermute | solution.py:410
  43.0 17.5 %collective-permute-start = (bf16[4,32,512]{2,1,0:T(8,128)(2,1)S(1)}, bf16[4,32,512]{2,1,0:T(8,128)(2,1)S(1)}, u32[]{:S(2)}, u32[]{:S(2)}) collective-permute-start(bf16[4,32,512]{2,1,0:T(8,128)(2,1)S(1)} %copy-done.7), channel_id=1, source_target_pairs={{0,1},{1,0},{2,3},{3,2},{4,5},{5,4},{6,7},{7,6},{8,9},{9,8},{10,11... | collective-permute-start | bytes 393224 | tf_op jit(solution)/shard_map/ppermute | solution.py:410
  43.1 17.5 %collective-permute-start.1 = (bf16[4,32,512]{2,1,0:T(8,128)(2,1)S(1)}, bf16[4,32,512]{2,1,0:T(8,128)(2,1)S(1)}, u32[]{:S(2)}, u32[]{:S(2)}) collective-permute-start(bf16[4,32,512]{2,1,0:T(8,128)(2,1)S(1)} %copy-done.6), channel_id=1, source_target_pairs={{1,2},{3,4},{5,6},{7,8},{9,10},{11,12},{13,14},{15,16},{17,18},{19... | collective-permute-start | bytes 393224 | tf_op jit(solution)/shard_map/ppermute | solution.py:418
  51.9 10.2 %collective-permute-start.7 = (bf16[4,32,128]{2,1,0:T(8,128)(2,1)S(1)}, bf16[4,32,128]{2,1,0:T(8,128)(2,1)S(1)}, u32[]{:S(2)}, u32[]{:S(2)}) collective-permute-start(bf16[4,32,128]{2,1,0:T(8,128)(2,1)S(1)} %get-tuple-element.28), channel_id=1, source_target_pairs={{0,16},{16,0},{32,48},{48,32},{64,80},{80,64},{96,112},{112,96},{1... | collective-permute-start | bytes 98312 | tf_op jit(solution)/shard_map/ppermute | solution.py:410
  52.0 10.1 %collective-permute-start.8 = (bf16[4,32,128]{2,1,0:T(8,128)(2,1)S(1)}, bf16[4,32,128]{2,1,0:T(8,128)(2,1)S(1)}, u32[]{:S(2)}, u32[]{:S(2)}) collective-permute-start(bf16[4,32,128]{2,1,0:T(8,128)(2,1)S(1)} %get-tuple-element.29), channel_id=1, source_target_pairs={{16,32},{48,64},{80,96},{112,128},{144,160},{176,192},{208,224},{3... | collective-permute-start | bytes 98312 | tf_op jit(solution)/shard_map/ppermute | solution.py:418
